TPU v7x, 256 devices: a whole 4x4x8 slice. The times are simulated.
256 devices in a mesh: seq: 32 (over x, z), chan: 8 (over y, core).
Axes of the slice: x: 4, y: 4, z: 8, core: 2. Of those that a mesh axis runs over, the one named last changes fastest.
Arguments:
- query_rows: bfloat16 [8192, 2048], P('seq', 'chan'), may hold values from -6 to 6
- key_rows: bfloat16 [8192, 2048], P('seq', 'chan'), may hold values from -6 to 6
- value_rows: bfloat16 [8192, 2048], P('seq', 'chan'), may hold values from -6 to 6
- long_filter: float32 [8192, 2048], P('seq', 'chan'), may hold values from -2 to 2
- short_taps: float32 [3, 3, 2048], P(None, None, ('seq', 'chan')), may hold values from -3 to 3
- skip_gain: float32 [2048], P(('seq', 'chan')), may hold values from -3 to 3
- cotangent: bfloat16 [8192, 2048], P('seq', 'chan'), may hold values from -6 to 6
Outputs:
- gated_out: bfloat16 [8192, 2048], P('seq', 'chan')
- query_grad: bfloat16 [8192, 2048], P('seq', 'chan')
- key_grad: bfloat16 [8192, 2048], P('seq', 'chan')
- value_grad: bfloat16 [8192, 2048], P('seq', 'chan')
- filter_grad: float32 [8192, 2048], P('seq', 'chan')
- taps_grad: float32 [3, 3, 2048], P(None, None, 'chan')
- skip_grad: float32 [2048], P('chan')
All inputs are finite; a program needn't handle non-finite values.
Results may differ from a plain program's by a relative error of at most 0.00135.
Values may be sent and summed in bfloat16 or wider, within the bound.
A program may use at most 64 MiB of HBM per device.

v0:
```python
import math

import jax
import jax.numpy as jnp
from jax import lax
from jax.sharding import PartitionSpec as P

exact_dot = lax.Precision.HIGHEST


def from_behind(value, axis, by):
    length = lax.axis_size(axis)
    pairs = [(i, i + by) for i in range(length) if 0 <= i + by < length]
    return lax.ppermute(value, axis, pairs)


def angles(left_index, right_index, period):
    product = left_index[:, None] * right_index[None, :] % period
    return 2.0 * math.pi / period * product.astype(jnp.float32)


def source_transform(pieces, row_start, total):
    sources = pieces.shape[1]
    row_count = pieces.shape[2]
    source_index = jnp.arange(sources, dtype=jnp.int32)
    freq_index = jnp.arange(2 * sources, dtype=jnp.int32)
    theta = angles(source_index, freq_index, 2 * sources)
    real_part = jnp.einsum("fqrc,qk->fkrc", pieces, jnp.cos(theta), precision=exact_dot)
    imag_part = -jnp.einsum("fqrc,qk->fkrc", pieces, jnp.sin(theta), precision=exact_dot)
    row_index = row_start + jnp.arange(row_count, dtype=jnp.int32)
    twist = angles(freq_index, row_index, total)
    cosine = jnp.cos(twist)[None, :, :, None]
    sine = jnp.sin(twist)[None, :, :, None]
    return jnp.stack([real_part * cosine + imag_part * sine, imag_part * cosine - real_part * sine])


def row_transform(spectra, direction):
    length = spectra.shape[3]
    positions = jnp.arange(length, dtype=jnp.int32)
    theta = angles(positions, positions, length)
    cosine = jnp.cos(theta)
    sine = jnp.sin(theta)
    real_cos = jnp.einsum("femc,mk->fekc", spectra[0], cosine, precision=exact_dot)
    real_sin = jnp.einsum("femc,mk->fekc", spectra[0], sine, precision=exact_dot)
    imag_cos = jnp.einsum("femc,mk->fekc", spectra[1], cosine, precision=exact_dot)
    imag_sin = jnp.einsum("femc,mk->fekc", spectra[1], sine, precision=exact_dot)
    return jnp.stack([real_cos - direction * imag_sin, imag_cos + direction * real_sin])


def untwist(spectra, freq_start, total):
    freq_index = freq_start + jnp.arange(spectra.shape[2], dtype=jnp.int32)
    row_index = jnp.arange(spectra.shape[3], dtype=jnp.int32)
    twist = angles(freq_index, row_index, total)
    cosine = jnp.cos(twist)[None, :, :, None]
    sine = jnp.sin(twist)[None, :, :, None]
    return jnp.stack(
        [spectra[0] * cosine - spectra[1] * sine, spectra[1] * cosine + spectra[0] * sine]
    )


def source_sum(spectra, total):
    freqs = spectra.shape[2]
    theta = angles(
        jnp.arange(freqs // 2, dtype=jnp.int32), jnp.arange(freqs, dtype=jnp.int32), freqs
    )
    summed = jnp.einsum("fkrc,qk->fqrc", spectra[0], jnp.cos(theta), precision=exact_dot)
    summed = summed - jnp.einsum("fkrc,qk->fqrc", spectra[1], jnp.sin(theta), precision=exact_dot)
    return summed / total


def spectrum_split(fields):
    devices = lax.axis_size("seq")
    place = lax.axis_index("seq")
    nfields, row_count, channels = fields.shape
    share = row_count // devices
    total = 2 * devices * row_count
    mixed = source_transform(
        lax.all_to_all(
            fields.reshape(nfields, 1, row_count, channels),
            "seq",
            split_axis=2,
            concat_axis=1,
            tiled=True,
        ),
        place * share,
        total,
    )
    mixed = mixed.reshape(2, nfields, devices, 2, share, channels)
    return row_transform(
        lax.all_to_all(mixed, "seq", split_axis=2, concat_axis=4, tiled=True)[:, :, 0], -1.0
    )


def signal_split(spectra):
    devices = lax.axis_size("seq")
    place = lax.axis_index("seq")
    nfields = spectra.shape[1]
    row_count = spectra.shape[3]
    channels = spectra.shape[4]
    share = row_count // devices
    total = 2 * devices * row_count
    turned = untwist(row_transform(spectra, 1.0), 2 * place, total)
    turned = turned.reshape(2, nfields, 1, 2, devices, share, channels)
    pieces = lax.all_to_all(turned, "seq", split_axis=4, concat_axis=2, tiled=True)
    gathered = source_sum(pieces.reshape(2, nfields, 2 * devices, share, pieces.shape[6]), total)
    return lax.all_to_all(gathered, "seq", split_axis=1, concat_axis=2, tiled=True).reshape(
        nfields, row_count, channels
    )


def complex_product(left, right, conjugate):
    right_imag = -right[1] if conjugate else right[1]
    return jnp.stack(
        [left[0] * right[0] - left[1] * right_imag, left[0] * right_imag + left[1] * right[0]]
    )


def per_device(query_rows, key_rows, value_rows, long_filter, short_taps, skip_gain, cotangent):
    row_count, channels = query_rows.shape
    devices = lax.axis_size("seq")
    grad_scale = 1.0 / math.sqrt(row_count * devices)
    all_taps, all_gain = (
        lax.all_gather(short_taps, ("seq", "chan"), axis=2, tiled=True),
        lax.all_gather(skip_gain, ("seq", "chan"), axis=0, tiled=True),
    )
    start = lax.axis_index("chan") * channels
    tap_block = lax.dynamic_slice_in_dim(all_taps, start, channels, 2)
    skip_block = lax.dynamic_slice_in_dim(all_gain, start, channels, 0)
    streams = jnp.stack([query_rows, key_rows, value_rows])
    lower = from_behind(streams[:, row_count - 2 :, :], "seq", 1)
    extended = jnp.concatenate([lower, streams], axis=1).astype(jnp.float32)
    shorted = sum(
        (
            tap_block[:, offset, None, :] * extended[:, 2 - offset : 2 - offset + row_count]
            for offset in range(3)
        )
    )
    query_conv = shorted[0]
    key_conv = shorted[1]
    value_conv = shorted[2]
    product = key_conv * value_conv
    upstream = cotangent.astype(jnp.float32)
    gated_grad = upstream * query_conv
    spectra = spectrum_split(jnp.stack([product, long_filter]))
    prod_spec = spectra[:, 0]
    filt_spec = spectra[:, 1]
    conv_part = signal_split(complex_product(prod_spec, filt_spec, False)[:, None])[0]
    grad_spec = spectrum_split(gated_grad[None])[:, 0]
    back = signal_split(
        jnp.stack(
            [
                complex_product(grad_spec, filt_spec, True),
                complex_product(grad_spec, prod_spec, True),
            ],
            axis=1,
        )
    )
    corr_product = back[0]
    corr_filter = back[1]
    mixed_conv = conv_part + skip_block * product
    gated_out = (query_conv * mixed_conv).astype(jnp.bfloat16)
    query_conv_grad = upstream * mixed_conv
    product_grad = corr_product + skip_block * gated_grad
    filter_grad = grad_scale * corr_filter
    key_conv_grad = product_grad * value_conv
    value_conv_grad = product_grad * key_conv
    conv_grads = jnp.stack([query_conv_grad, key_conv_grad, value_conv_grad])
    upper = from_behind(conv_grads[:, :2, :], "seq", -1)
    ext_grads = jnp.concatenate([conv_grads, upper], axis=1)
    input_grads = sum(
        (
            tap_block[:, offset, None, :] * ext_grads[:, offset : offset + row_count]
            for offset in range(3)
        )
    ).astype(jnp.bfloat16)
    tap_terms = jnp.stack(
        [
            jnp.sum(conv_grads * extended[:, 2 - offset : 2 - offset + row_count], axis=1)
            for offset in range(3)
        ],
        axis=1,
    )
    skip_terms = jnp.sum(gated_grad * product, axis=0)
    tap_total, skip_total = lax.psum((tap_terms, skip_terms), "seq")
    return (
        gated_out,
        input_grads[0],
        input_grads[1],
        input_grads[2],
        filter_grad,
        grad_scale * tap_total,
        grad_scale * skip_total,
    )


def solution(mesh):
    in_specs = (
        P("seq", "chan"),
        P("seq", "chan"),
        P("seq", "chan"),
        P("seq", "chan"),
        P(None, None, ("seq", "chan")),
        P(("seq", "chan")),
        P("seq", "chan"),
    )
    out_specs = (
        P("seq", "chan"),
        P("seq", "chan"),
        P("seq", "chan"),
        P("seq", "chan"),
        P("seq", "chan"),
        P(None, None, "chan"),
        P("chan"),
    )
    return jax.shard_map(
        per_device, mesh=mesh, in_specs=in_specs, out_specs=out_specs, check_vma=False
    )
```

profile of v0, /device:TPU:16, one launch (start us, length us, event | category | flops | bytes accessed | tf_op | source)
XLA Modules:
  0.0 596.4 jit_solution(4957405621104877456)
XLA Ops:
  1.4 3.8 collective-permute-start
  6.0 83.7 %all_gather.6 = f32[3,3,2048]{1,0,2:T(4,128)} all-gather(f32[3,3,8]{1,0,2:T(4,128)S(1)} %copy.38), channel_id=1, replica_groups=mesh['seq'=32,'chan'=8] {'seq','chan'}, dimensions={2}, use_global_device_ids=true | all-gather | bytes 74016 | tf_op jit(solution)/shard_map/all_gather | solution.py:123
  89.7 2.2 constant_dynamic-slice_fusion.1
  94.4 7.1 %all-to-all-start.4 = ((f32[1,1,256,256]{3,1,0,2:T(1,128)}), f32[1,1,256,256]{3,1,0,2:T(1,128)S(1)}, u32[]{:S(2)}, u32[]{:S(2)}) async-start(f32[1,1,256,256]{3,1,0,2:T(1,128)} %copy.55), calls=%async_computation.4 | async-start | bytes 524288 | tf_op jit(solution)/shard_map/all_to_all | solution.py:78
  102.8 11.3 %all-to-all-done.4 = f32[1,1,256,256]{3,1,0,2:T(1,128)S(1)} async-done(((f32[1,1,256,256]{3,1,0,2:T(1,128)}), f32[1,1,256,256]{3,1,0,2:T(1,128)S(1)}, u32[]{:S(2)}, u32[]{:S(2)}) %all-to-all-start.4) | async-done | bytes 262176 | tf_op jit(solution)/shard_map/all_to_all | solution.py:78
  114.1 4.7 all-to-all-start
  121.7 1.6 copy.78
  123.3 12.5 %all-to-all-done = f32[2,1,256,256]{3,0,1,2:T(2,128)S(1)} async-done(((f32[2,1,256,256]{3,0,1,2:T(2,128)}), f32[2,1,256,256]{3,0,1,2:T(2,128)S(1)}, u32[]{:S(2)}, u32[]{:S(2)}) %all-to-all-start) | async-done | bytes 524320 | tf_op jit(solution)/shard_map/all_to_all | solution.py:78
  135.8 5.8 all-to-all-start.5
  144.1 1.6 stack.117
  145.6 1.6 stack.118
  147.2 2.7 pad_maximum_fusion
  150.0 2.5 copy.74
  152.5 17.1 %all-to-all-done.5 = f32[2,1,32,2,8,256]{5,3,4,1,0,2:T(2,128)} async-done(((f32[2,1,32,2,8,256]{5,3,4,1,0,2:T(2,128)}), f32[2,1,32,2,8,256]{5,3,4,1,0,2:T(2,128)}, u32[]{:S(2)}, u32[]{:S(2)}) %all-to-all-start.5) | async-done | bytes 1048608 | tf_op jit(solution)/shard_map/all_to_all | solution.py:90
  169.7 4.9 all-to-all-start.1
  174.7 2.4 fusion.254
  177.1 47.1 %all-to-all-done.1 = f32[2,2,32,2,8,256]{5,3,4,1,0,2:T(2,128)S(1)} async-done(((f32[2,2,32,2,8,256]{5,3,4,1,0,2:T(2,128)}), f32[2,2,32,2,8,256]{5,3,4,1,0,2:T(2,128)S(1)}, u32[]{:S(2)}, u32[]{:S(2)}) %all-to-all-start.1) | async-done | bytes 2097184 | tf_op jit(solution)/shard_map/all_to_all | solution.py:90
  225.0 2.0 fusion.23
  227.1 2.0 fusion.19
  229.1 2.1 fusion.5
  231.2 2.1 fusion.3
  233.4 1.6 fusion.45
  235.1 13.2 %fusion.49 = f32[256,2,256]{2,0,1:T(8,128)S(1)} fusion(f32[1,1,2,256,256]{4,3,2,1,0:T(8,128)S(1)} %get-tuple-element.40), kind=kOutput, calls=%fused_computation.91 | convolution fusion | flops 403570688 | bytes 1048576 | tf_op jit(solution)/shard_map/femc,mk->fekc/dot_general | solution.py:43
  248.3 1.6 fusion.12
  249.9 1.8 subtract_bitcast_fusion.2
  252.9 6.2 %all-to-all-start.2 = ((f32[2,1,1,2,32,8,256]{6,5,3,2,1,0,4:T(8,128)}), f32[2,1,1,2,32,8,256]{6,5,3,2,1,0,4:T(8,128)}, u32[]{:S(2)}, u32[]{:S(2)}) async-start(f32[2,1,1,2,32,8,256]{6,5,3,2,1,0,4:T(8,128)} %copy.75), calls=%async_computation.2 | async-start | bytes 2097152 | tf_op jit(solution)/shard_map/all_to_all | solution.py:104
  259.1 1.6 fusion.40
  260.7 2.7 fusion.11
  263.4 1.6 fusion.36
  265.1 2.0 fusion.32
  267.2 2.0 fusion.58
  269.2 2.0 fusion.79
  271.3 2.3 fusion
  273.6 2.3 subtract_bitcast_fusion
  276.0 1.6 copy.79
  277.6 9.7 %all-to-all-done.2 = f32[2,1,1,2,32,8,256]{6,5,3,2,1,0,4:T(8,128)} async-done(((f32[2,1,1,2,32,8,256]{6,5,3,2,1,0,4:T(8,128)}), f32[2,1,1,2,32,8,256]{6,5,3,2,1,0,4:T(8,128)}, u32[]{:S(2)}, u32[]{:S(2)}) %all-to-all-start.2) | async-done | bytes 1048608 | tf_op jit(solution)/shard_map/all_to_all | solution.py:104
  287.4 4.9 all-to-all-start.6
  295.6 46.4 %all-to-all-done.6 = f32[2,2,1,2,32,8,256]{6,5,3,1,2,0,4:T(8,128)S(1)} async-done(((f32[2,2,1,2,32,8,256]{6,5,3,1,2,0,4:T(8,128)}), f32[2,2,1,2,32,8,256]{6,5,3,1,2,0,4:T(8,128)S(1)}, u32[]{:S(2)}, u32[]{:S(2)}) %all-to-all-start.6) | async-done | bytes 2097184 | tf_op jit(solution)/shard_map/all_to_all | solution.py:104
  342.0 6.0 %all-to-all-start.3 = ((f32[1,32,8,256]{3,2,0,1:T(8,128)}), f32[1,32,8,256]{3,2,0,1:T(8,128)S(1)}, u32[]{:S(2)}, u32[]{:S(2)}) async-start(f32[1,32,8,256]{3,2,0,1:T(8,128)} %copy.54), calls=%async_computation.3 | async-start | bytes 524288 | tf_op jit(solution)/shard_map/all_to_all | solution.py:106
  349.2 1.5 copy.65
  350.6 1.9 squeeze.40
  352.6 2.7 copy.64
  355.3 2.9 squeeze.39
  358.2 1.9 fusion.118
  362.0 9.8 %all-to-all-start.7 = ((f32[2,32,8,256]{3,2,0,1:T(8,128)}), f32[2,32,8,256]{3,2,0,1:T(8,128)S(1)}, u32[]{:S(2)}, u32[]{:S(2)}) async-start(f32[2,32,8,256]{3,2,0,1:T(8,128)} %copy.66), calls=%async_computation.7 | async-start | bytes 1048576 | tf_op jit(solution)/shard_map/all_to_all | solution.py:106
  372.1 75.7 %all-reduce = f32[2048]{0:T(1024)S(1)} all-reduce(f32[2048]{0:T(1024)S(1)} %dynamic-update-slice), channel_id=1, replica_groups=mesh['seq'=32,'chan'=8] {'seq','chan'}, use_global_device_ids=true, to_apply=%add | all-reduce | flops 2048 | bytes 16384
  450.8 3.5 collective-permute-done.1
  454.9 139.2 %all-reduce.1 = (f32[3,3,256]{2,0,1:T(4,128)S(1)}, f32[256]{0:T(256)S(1)}) all-reduce(f32[3,3,256]{2,0,1:T(4,128)S(1)} %pad_maximum_fusion.7, f32[256]{0:T(256)S(1)} %get-tuple-element.57), channel_id=1, replica_groups=mesh['seq'=32,'chan'=8] {'seq'}, use_global_device_ids=true, to_apply=%region_3.4 | all-reduce | flops 2560 | bytes 20480 | tf_op jit(solution)/shard_map/psum | solution.py:184
  (78 shorter events, 25.2 us)
Async XLA Ops:
  1.4 91.1 %collective-permute-start = (bf16[3,2,256]{2,1,0:T(2,128)(2,1)S(1)}, bf16[3,2,256]{2,1,0:T(2,128)(2,1)S(1)}, u32[]{:S(2)}, u32[]{:S(2)}) collective-permute-start(bf16[3,2,256]{2,1,0:T(2,128)(2,1)S(1)} %pad_maximum_fusion.8), channel_id=1, source_target_pairs={{0,8},{8,16},{16,24},{24,32},{32,40},{40,48},{48,56},{56,64},{64,7... | collective-permute-start | bytes 9224 | tf_op jit(solution)/shard_map/ppermute | solution.py:14
  89.6 2.8 copy-start.4
  89.6 2.8 copy-start.5
  89.7 2.8 copy-start.6
  92.5 0.9 copy-start.7
  92.6 8.9 %copy-start.9 = (f32[256,256]{1,0:T(8,128)S(1)}, f32[256,256]{1,0:T(8,128)}, u32[]{:S(2)}) copy-start(f32[256,256]{1,0:T(8,128)} %param.10) | copy-start | bytes 786436
  93.4 9.4 %copy-start = (f32[3,256,256]{2,1,0:T(8,128)}, f32[3,256,256]{2,1,0:T(8,128)S(1)}, u32[]{:S(2)}) copy-start(f32[3,256,256]{2,1,0:T(8,128)S(1)} %multiply_add_fusion) | copy-start | bytes 2359300
  94.4 19.7 %all-to-all-start.4 = ((f32[1,1,256,256]{3,1,0,2:T(1,128)}), f32[1,1,256,256]{3,1,0,2:T(1,128)S(1)}, u32[]{:S(2)}, u32[]{:S(2)}) async-start(f32[1,1,256,256]{3,1,0,2:T(1,128)} %copy.55), calls=%async_computation.4 | async-start | bytes 524288 | tf_op jit(solution)/shard_map/all_to_all | solution.py:78
  114.1 21.6 %all-to-all-start = ((f32[2,1,256,256]{3,0,1,2:T(2,128)}), f32[2,1,256,256]{3,0,1,2:T(2,128)S(1)}, u32[]{:S(2)}, u32[]{:S(2)}) async-start(f32[2,1,256,256]{3,0,1,2:T(2,128)} %copy.42), calls=%async_computation | async-start | bytes 1048576 | tf_op jit(solution)/shard_map/all_to_all | solution.py:78
  135.8 33.9 %all-to-all-start.5 = ((f32[2,1,32,2,8,256]{5,3,4,1,0,2:T(2,128)}), f32[2,1,32,2,8,256]{5,3,4,1,0,2:T(2,128)}, u32[]{:S(2)}, u32[]{:S(2)}) async-start(f32[2,1,32,2,8,256]{5,3,4,1,0,2:T(2,128)} %copy.78), calls=%async_computation.5 | async-start | bytes 2097152 | tf_op jit(solution)/shard_map/all_to_all | solution.py:90
  145.6 1.6 copy-start.2
  169.7 54.5 %all-to-all-start.1 = ((f32[2,2,32,2,8,256]{5,3,4,1,0,2:T(2,128)}), f32[2,2,32,2,8,256]{5,3,4,1,0,2:T(2,128)S(1)}, u32[]{:S(2)}, u32[]{:S(2)}) async-start(f32[2,2,32,2,8,256]{5,3,4,1,0,2:T(2,128)} %copy.74), calls=%async_computation.1 | async-start | bytes 4194304 | tf_op jit(solution)/shard_map/all_to_all | solution.py:90
  252.9 34.5 %all-to-all-start.2 = ((f32[2,1,1,2,32,8,256]{6,5,3,2,1,0,4:T(8,128)}), f32[2,1,1,2,32,8,256]{6,5,3,2,1,0,4:T(8,128)}, u32[]{:S(2)}, u32[]{:S(2)}) async-start(f32[2,1,1,2,32,8,256]{6,5,3,2,1,0,4:T(8,128)} %copy.75), calls=%async_computation.2 | async-start | bytes 2097152 | tf_op jit(solution)/shard_map/all_to_all | solution.py:104
  259.1 4.3 copy-start.3
  287.4 54.6 %all-to-all-start.6 = ((f32[2,2,1,2,32,8,256]{6,5,3,1,2,0,4:T(8,128)}), f32[2,2,1,2,32,8,256]{6,5,3,1,2,0,4:T(8,128)S(1)}, u32[]{:S(2)}, u32[]{:S(2)}) async-start(f32[2,2,1,2,32,8,256]{6,5,3,1,2,0,4:T(8,128)} %copy.79), calls=%async_computation.6 | async-start | bytes 4194304 | tf_op jit(solution)/shard_map/all_to_all | solution.py:104
  342.0 20.1 %all-to-all-start.3 = ((f32[1,32,8,256]{3,2,0,1:T(8,128)}), f32[1,32,8,256]{3,2,0,1:T(8,128)S(1)}, u32[]{:S(2)}, u32[]{:S(2)}) async-start(f32[1,32,8,256]{3,2,0,1:T(8,128)} %copy.54), calls=%async_computation.3 | async-start | bytes 524288 | tf_op jit(solution)/shard_map/all_to_all | solution.py:106
  360.2 11.7 %copy-start.10 = (f32[8]{0:T(128)S(1)}, f32[8]{0:T(128)}, u32[]{:S(2)}) copy-start(f32[8]{0:T(128)} %param.12) | copy-start | bytes 100
  360.2 87.7 %copy-start.1 = (f32[3,256,256]{2,1,0:T(8,128)S(1)}, f32[3,256,256]{2,1,0:T(8,128)}, u32[]{:S(2)}) copy-start(f32[3,256,256]{2,1,0:T(8,128)} %copy-done) | copy-start | bytes 2359300
  360.2 87.7 %copy-start.8 = (bf16[256,256]{1,0:T(8,128)(2,1)S(1)}, bf16[256,256]{1,0:T(8,128)(2,1)}, u32[]{:S(2)}) copy-start(bf16[256,256]{1,0:T(8,128)(2,1)} %param.13) | copy-start | bytes 393220
  362.0 85.9 %all-to-all-start.7 = ((f32[2,32,8,256]{3,2,0,1:T(8,128)}), f32[2,32,8,256]{3,2,0,1:T(8,128)S(1)}, u32[]{:S(2)}, u32[]{:S(2)}) async-start(f32[2,32,8,256]{3,2,0,1:T(8,128)} %copy.66), calls=%async_computation.7 | async-start | bytes 1048576 | tf_op jit(solution)/shard_map/all_to_all | solution.py:106
  448.8 5.5 collective-permute-start.1
where the time goes:
time: 606 us; the launch traced here: 596 us
  blocking collectives  299 us (49%)
  waiting for transfers between devices  148 us (24%)
  starting transfers between devices  54.4 us (9%)
  matrix products  50.8 us (8%)
  local copies, waits for them, and re-layouts  35.5 us (6%)
  other arithmetic  7.9 us (1%)
    psum x1, blocking collectives, per_device(): tap_total, skip_total = lax.psum((tap_terms, skip_terms), 'seq')  139 us
    all_gather x1, blocking collectives, per_device(): lax.all_gather(short_taps, ('seq', 'chan'), axis=2, tiled=True)  83.7 us
    unnamed x1, blocking collectives  75.7 us
    all_to_all x2, waiting for transfers between devices, spectrum_split(): lax.all_to_all(mixed, 'seq', split_axis=2, concat_axis=4, tiled=True)  64.2 us
    all_to_all x2, waiting for transfers between devices, signal_split(): lax.all_to_all(turned, 'seq', split_axis=4, concat_axis=2, tiled=True)  56.1 us
    all_to_all x2, waiting for transfers between devices, spectrum_split(): lax.all_to_all(fields.reshape(nfields, 1, row_count, channels), 'seq', sp...  23.8 us
    dot_general x4, matrix products, row_transform(): jnp.einsum('femc,mk->fekc', spectra[0], cosine, precision=exact_dot)  18.9 us
    all_to_all x2, starting transfers between devices, signal_split(): lax.all_to_all(gathered, 'seq', split_axis=1, concat_axis=2, tiled=True)  15.8 us
  transfers between devices with their start and end apart: 10, of which 7 were waited for; matrix products, arithmetic and copies ran while one was open for 10% of the time, Pallas kernels for 0%

commit v1 on v0

v1 whole, which is shorter than its diff:
```python
import functools
import math

import jax
import jax.numpy as jnp
import ml_dtypes
import numpy as np
from jax import lax
from jax.experimental import pallas as pl
from jax.experimental.pallas import tpu as pltpu
from jax.sharding import PartitionSpec as P

F32 = jnp.float32
BF16 = jnp.bfloat16
MESH = pl.DeviceIdType.MESH


def halves(table):
    high = table.astype(np.float32).astype(ml_dtypes.bfloat16)
    low = (table - high.astype(np.float64)).astype(np.float32).astype(ml_dtypes.bfloat16)
    return np.stack([high, low])


def transform_tables(blocks, width, group):
    total = blocks * width
    shifted = np.arange(blocks) - 0.25
    outer = 2.0 * np.pi / blocks * np.outer(shifted, np.arange(blocks))
    eye = np.eye(group)
    left = np.concatenate([np.kron(np.cos(outer), eye), np.kron(-np.sin(outer), eye)], axis=0)
    back = left.T / total
    inner = 2.0 * np.pi / width * (np.outer(np.arange(width), np.arange(width)) % width)
    right = np.stack([halves(np.cos(inner)), halves(np.sin(inner))])
    turn = 2.0 * np.pi / total * np.outer(shifted, np.arange(width))
    twist = np.stack([np.cos(turn), np.sin(turn)]).astype(np.float32)
    twist = np.repeat(twist, group, axis=1)
    return halves(left), halves(back), right, twist


def split(value):
    high = value.astype(BF16)
    return high, (value - high.astype(F32)).astype(BF16)


def dot(left, right):
    return jnp.dot(left, right, preferred_element_type=F32)


def dot3(left, right):
    return dot(left[0], right[0]) + dot(left[0], right[1]) + dot(left[1], right[0])


def delayed(value, steps):
    before = jnp.concatenate([jnp.zeros_like(value[:1]), value[:-1]], axis=0)
    lane = lax.broadcasted_iota(jnp.int32, value.shape, 2)
    return jnp.where(
        lane < steps, pltpu.roll(before, steps, 2), pltpu.roll(value, steps, 2)
    )


def advanced(value, steps):
    width = value.shape[2]
    after = jnp.concatenate([value[1:], jnp.zeros_like(value[:1])], axis=0)
    lane = lax.broadcasted_iota(jnp.int32, value.shape, 2)
    return jnp.where(
        lane >= width - steps,
        pltpu.roll(after, width - steps, 2),
        pltpu.roll(value, width - steps, 2),
    )


def total_of(value):
    return jnp.sum(jnp.sum(value, axis=0), axis=1, keepdims=True)


def kernel(
    nseq,
    nchan,
    group,
    scale,
    q_ref,
    k_ref,
    v_ref,
    c_ref,
    h_ref,
    side_ref,
    left_hbm,
    back_hbm,
    right_hbm,
    twist_hbm,
    go_ref,
    qg_ref,
    kg_ref,
    vg_ref,
    fg_ref,
    sums_ref,
    left,
    back,
    right,
    twist,
    send_h,
    send_kv,
    send_qc,
    got_h,
    got_kv,
    got_qc,
    side,
    out_gq,
    out_f,
    out_kv,
    out_s,
    in_gq,
    in_f,
    in_kv,
    in_s,
    x_q,
    x_k,
    x_v,
    x_c,
    x_p,
    x_g,
    d_q,
    d_k,
    d_v,
    spec_h,
    spec_p,
    spec_g,
    table_sem,
    send_sem,
    recv_sem,
    side_sem,
):
    me = lax.axis_index("seq")
    mine = lax.axis_index("chan")
    rows, width = q_ref.shape

    tables = [
        pltpu.make_async_copy(src, dst, table_sem.at[i])
        for i, (src, dst) in enumerate(
            [(left_hbm, left), (back_hbm, back), (right_hbm, right), (twist_hbm, twist)]
        )
    ]
    for copy in tables:
        copy.start()

    per = nseq // nchan
    to_seq = nchan * lax.rem(me, per) + mine
    to_chan = lax.div(me, per)
    from_seq = per * mine + lax.div(me, nchan)
    from_chan = lax.rem(me, nchan)
    stays = jnp.logical_and(to_seq == me, to_chan == mine)

    barrier = pltpu.get_barrier_semaphore()

    def greet(step, carry):
        peer = lax.rem(me + step, nseq)
        pl.semaphore_signal(barrier, inc=1, device_id=(peer, mine), device_id_type=MESH)
        return carry

    lax.fori_loop(1, nseq, greet, 0)

    @pl.when(jnp.logical_not(stays))
    def _():
        pl.semaphore_signal(
            barrier, inc=1, device_id=(from_seq, from_chan), device_id_type=MESH
        )

    send_h[...] = h_ref[...].T.reshape(nseq, group, width)

    @pl.when(stays)
    def _():
        pl.semaphore_wait(barrier, nseq - 1)

    @pl.when(jnp.logical_not(stays))
    def _():
        pl.semaphore_wait(barrier, nseq)

    def copy_to(source, target, index, peer):
        return pltpu.make_async_remote_copy(
            src_ref=source.at[peer],
            dst_ref=target.at[me],
            send_sem=send_sem.at[index],
            recv_sem=recv_sem.at[index],
            device_id=(peer, mine),
            device_id_type=MESH,
        )

    def send_all(source, target, index):
        def body(step, carry):
            copy_to(source, target, index, lax.rem(me + step, nseq)).start()
            return carry

        lax.fori_loop(1, nseq, body, 0)
        target[me] = source[me]

    def arrived(target, index):
        part = target.at[pl.ds(0, nseq - 1)]
        pltpu.make_async_copy(part, part, recv_sem.at[index]).wait()

    def sent(source, index):
        part = source.at[pl.ds(0, nseq - 1)]
        pltpu.make_async_copy(part, part, send_sem.at[index]).wait()

    send_all(send_h, got_h, 0)

    side_copy = pltpu.make_async_remote_copy(
        src_ref=side_ref,
        dst_ref=side,
        send_sem=side_sem.at[0],
        recv_sem=side_sem.at[1],
        device_id=(to_seq, to_chan),
        device_id_type=MESH,
    )

    @pl.when(jnp.logical_not(stays))
    def _():
        side_copy.start()

    @pl.when(stays)
    def _():
        side[...] = side_ref[...]

    def paired(first, second):
        shape = (nseq, group, width)
        one = first[...].astype(F32).T.reshape(shape)
        two = second[...].astype(F32).T.reshape(shape)
        return jnp.concatenate([one, two], axis=1).astype(BF16)

    send_kv[...] = paired(k_ref, v_ref)
    send_all(send_kv, got_kv, 1)
    send_qc[...] = paired(q_ref, c_ref)
    send_all(send_qc, got_qc, 2)

    for copy in tables:
        copy.wait()

    def forward(signal, spec):
        parts = split(signal.reshape(rows, width))
        wave = dot3((left[0], left[1]), parts)
        real, imag = wave[:rows], wave[rows:]
        cosine, sine = twist[0], twist[1]
        turned_real = split(real * cosine + imag * sine)
        turned_imag = split(imag * cosine - real * sine)
        cos_parts = (right[0, 0], right[0, 1])
        sin_parts = (right[1, 0], right[1, 1])
        spec[0] = dot3(turned_real, cos_parts) + dot3(turned_imag, sin_parts)
        spec[1] = dot3(turned_imag, cos_parts) - dot3(turned_real, sin_parts)

    def inverse(real, imag):
        real, imag = split(real), split(imag)
        cos_parts = (right[0, 0], right[0, 1])
        sin_parts = (right[1, 0], right[1, 1])
        wave_real = dot3(real, cos_parts) - dot3(imag, sin_parts)
        wave_imag = dot3(imag, cos_parts) + dot3(real, sin_parts)
        cosine, sine = twist[0], twist[1]
        turned_real = split(wave_real * cosine - wave_imag * sine)
        turned_imag = split(wave_imag * cosine + wave_real * sine)
        signal = dot3((back[0, :, :rows], back[1, :, :rows]), turned_real)
        signal = signal + dot3((back[0, :, rows:], back[1, :, rows:]), turned_imag)
        return signal.reshape(nseq, group, width)

    arrived(got_h, 0)
    forward(got_h[...], spec_h)

    @pl.when(jnp.logical_not(stays))
    def _():
        side_copy.wait()

    taps = [[side[:, 3 * s + i : 3 * s + i + 1] for i in range(3)] for s in range(3)]
    gain = side[:, 9:10]

    def short(value, keep, coeffs):
        one, two = delayed(value, 1), delayed(value, 2)
        keep[0] = one
        keep[1] = two
        return coeffs[0] * value + coeffs[1] * one + coeffs[2] * two

    arrived(got_kv, 1)
    both = got_kv[...].astype(F32)
    x_k[...] = both[:, :group]
    x_v[...] = both[:, group:]
    key_conv = short(x_k[...], d_k, taps[1])
    value_conv = short(x_v[...], d_v, taps[2])
    x_p[...] = key_conv * value_conv
    forward(x_p[...], spec_p)
    h_re, h_im = spec_h[0], spec_h[1]
    p_re, p_im = spec_p[0], spec_p[1]
    mixed = inverse(p_re * h_re - p_im * h_im, p_re * h_im + p_im * h_re)
    mixed = mixed + gain * x_p[...]

    arrived(got_qc, 2)
    both = got_qc[...].astype(F32)
    x_q[...] = both[:, :group]
    x_c[...] = both[:, group:]
    query_conv = short(x_q[...], d_q, taps[0])
    x_g[...] = x_c[...] * query_conv
    query_conv_grad = x_c[...] * mixed

    def spread(grad, coeffs):
        return (
            coeffs[0] * grad + coeffs[1] * advanced(grad, 1) + coeffs[2] * advanced(grad, 2)
        )

    out_gq[...] = jnp.concatenate(
        [query_conv * mixed, spread(query_conv_grad, taps[0])], axis=1
    ).astype(BF16)
    send_all(out_gq, in_gq, 3)
    sums = [
        total_of(query_conv_grad * x_q[...]),
        total_of(query_conv_grad * d_q[0]),
        total_of(query_conv_grad * d_q[1]),
    ]

    forward(x_g[...], spec_g)
    g_re, g_im = spec_g[0], spec_g[1]
    p_re, p_im = spec_p[0], spec_p[1]
    out_f[...] = scale * inverse(p_re * g_re + p_im * g_im, p_re * g_im - p_im * g_re)
    send_all(out_f, in_f, 4)
    h_re, h_im = spec_h[0], spec_h[1]
    product_grad = inverse(h_re * g_re + h_im * g_im, h_re * g_im - h_im * g_re)
    product_grad = product_grad + gain * x_g[...]

    key_conv = taps[1][0] * x_k[...] + taps[1][1] * d_k[0] + taps[1][2] * d_k[1]
    value_conv = taps[2][0] * x_v[...] + taps[2][1] * d_v[0] + taps[2][2] * d_v[1]
    key_conv_grad = product_grad * value_conv
    value_conv_grad = product_grad * key_conv
    out_kv[...] = jnp.concatenate(
        [spread(key_conv_grad, taps[1]), spread(value_conv_grad, taps[2])], axis=1
    ).astype(BF16)
    send_all(out_kv, in_kv, 5)
    sums += [
        total_of(key_conv_grad * x_k[...]),
        total_of(key_conv_grad * d_k[0]),
        total_of(key_conv_grad * d_k[1]),
        total_of(value_conv_grad * x_v[...]),
        total_of(value_conv_grad * d_v[0]),
        total_of(value_conv_grad * d_v[1]),
        total_of(x_g[...] * x_p[...]),
    ]
    lane = lax.broadcasted_iota(jnp.int32, (group, 128), 1)
    place = lax.broadcasted_iota(jnp.int32, (group, 128), 0)
    packed = jnp.zeros((group, 128), F32)
    for index, value in enumerate(sums):
        packed = jnp.where(lane == group * index + place, value, packed)
    packed = scale * jnp.sum(packed, axis=0, keepdims=True)
    out_s[...] = jnp.broadcast_to(packed[None], out_s.shape)
    send_all(out_s, in_s, 6)

    def unpaired(source, first, second):
        both = source[...].astype(F32)
        first[...] = both[:, :group].reshape(rows, width).T.astype(BF16)
        second[...] = both[:, group:].reshape(rows, width).T.astype(BF16)

    arrived(in_gq, 3)
    unpaired(in_gq, go_ref, qg_ref)
    arrived(in_f, 4)
    fg_ref[...] = in_f[...].reshape(rows, width).T
    arrived(in_kv, 5)
    unpaired(in_kv, kg_ref, vg_ref)
    arrived(in_s, 6)
    sums_ref[...] = in_s[...]

    for index, source in enumerate([send_h, send_kv, send_qc, out_gq, out_f, out_kv, out_s]):
        sent(source, index)


def per_device(query_rows, key_rows, value_rows, long_filter, short_taps, skip_gain, cotangent):
    rows, channels = query_rows.shape
    nseq, nchan = lax.axis_size("seq"), lax.axis_size("chan")
    group = channels // nseq
    scale = 1.0 / math.sqrt(rows * nseq)
    tables = [jnp.asarray(t) for t in transform_tables(nseq, rows, group)]
    side = jnp.concatenate([short_taps.reshape(9, group), skip_gain.reshape(1, group)], axis=0)
    side = jnp.pad(side.T, ((0, 0), (0, 128 - 10)))
    block = jax.ShapeDtypeStruct((rows, channels), BF16)
    vmem = pl.BlockSpec(memory_space=pltpu.VMEM)
    hbm = pl.BlockSpec(memory_space=pl.ANY)
    one, two = (nseq, group, rows), (nseq, 2 * group, rows)
    spec = pltpu.VMEM((2, nseq * group, rows), F32)
    outs = pl.pallas_call(
        functools.partial(kernel, nseq, nchan, group, scale),
        out_shape=(
            block,
            block,
            block,
            block,
            jax.ShapeDtypeStruct((rows, channels), F32),
            jax.ShapeDtypeStruct((nseq, 1, 128), F32),
        ),
        in_specs=[vmem] * 6 + [hbm] * 4,
        out_specs=[vmem] * 6,
        scratch_shapes=[pltpu.VMEM(t.shape, t.dtype) for t in tables]
        + [
            pltpu.VMEM(one, F32),
            pltpu.VMEM(two, BF16),
            pltpu.VMEM(two, BF16),
            pltpu.VMEM(one, F32),
            pltpu.VMEM(two, BF16),
            pltpu.VMEM(two, BF16),
            pltpu.VMEM((group, 128), F32),
            pltpu.VMEM(two, BF16),
            pltpu.VMEM(one, F32),
            pltpu.VMEM(two, BF16),
            pltpu.VMEM((nseq, 1, 128), F32),
            pltpu.VMEM(two, BF16),
            pltpu.VMEM(one, F32),
            pltpu.VMEM(two, BF16),
            pltpu.VMEM((nseq, 1, 128), F32),
        ]
        + [pltpu.VMEM(one, F32)] * 6
        + [pltpu.VMEM((2,) + one, F32)] * 3
        + [spec] * 3
        + [
            pltpu.SemaphoreType.DMA((4,)),
            pltpu.SemaphoreType.DMA((7,)),
            pltpu.SemaphoreType.DMA((7,)),
            pltpu.SemaphoreType.DMA((2,)),
        ],
        compiler_params=pltpu.CompilerParams(
            collective_id=0, has_side_effects=True, vmem_limit_bytes=48 << 20
        ),
        name="hyena",
    )(query_rows, key_rows, value_rows, cotangent, long_filter, side, *tables)
    sums = outs[5].reshape(nseq, 128)[:, : 10 * group].reshape(nseq, 10, group)
    sums = sums.transpose(1, 0, 2).reshape(10, channels)
    return outs[:5] + (sums[:9].reshape(3, 3, channels), sums[9])


def solution(mesh):
    in_specs = (
        P("seq", "chan"),
        P("seq", "chan"),
        P("seq", "chan"),
        P("seq", "chan"),
        P(None, None, ("seq", "chan")),
        P(("seq", "chan")),
        P("seq", "chan"),
    )
    out_specs = (
        P("seq", "chan"),
        P("seq", "chan"),
        P("seq", "chan"),
        P("seq", "chan"),
        P("seq", "chan"),
        P(None, None, "chan"),
        P("chan"),
    )
    return jax.shard_map(
        per_device, mesh=mesh, in_specs=in_specs, out_specs=out_specs, check_vma=False
    )
```

time: 606 us -> 69.2 us (0.11); the launches traced: 596 us -> 68.8 us
  blocking collectives: 299 us -> 0 us
  waiting for transfers between devices: 148 us -> 0 us
  starting transfers between devices: 54.4 us -> 0 us
  Pallas kernels: 0 us -> 53.5 us
  matrix products: 50.8 us -> 0 us
  local copies, waits for them, and re-layouts: 35.5 us -> 14.5 us
  other arithmetic: 7.9 us -> 0.08 us
    all_to_all x8 -> x0, waiting for transfers between devices: 144 us -> none  [the longest x2 64.2 us: spectrum_split(): lax.all_to_all(mixed, 'seq', split_axis=2, concat_axis=4, tiled=True)]
    psum x1 -> x0, blocking collectives: 139 us -> none  [per_device(): tap_total, skip_total = lax.psum((tap_terms, skip_terms), 'seq')]
    all_gather x1 -> x0, blocking collectives: 83.7 us -> none  [per_device(): lax.all_gather(short_taps, ('seq', 'chan'), axis=2, tiled=True)]
    unnamed x1 -> x0, blocking collectives: 75.7 us -> none
    pallas_call x0 -> x1, Pallas kernels: none -> 53.5 us  [per_device(): pl.pallas_call(functools.partial(kernel, nseq, nchan, group, scale), out_...]
    dot_general x24 -> x0, matrix products: 50.8 us -> none  [the longest x4 18.9 us: row_transform(): jnp.einsum('femc,mk->fekc', spectra[0], cosine, precision=exact_dot)]
    all_to_all x8 -> x0, starting transfers between devices: 49.3 us -> none  [the longest x2 15.8 us: signal_split(): lax.all_to_all(gathered, 'seq', split_axis=1, concat_axis=2, tiled=True)]
    slice x11 -> x5, local copies, waits for them, and re-layouts: 12.7 us -> 0.27 us  [the longest x4 0.18 us: per_device(): return outs[:5] + (sums[:9].reshape(3, 3, channels), sums[9])]
  transfers between devices with their start and end apart: 10 -> 0, of which waited for: 7 -> 0; matrix products, arithmetic and copies ran while one was open for 10% -> 0% of each run, Pallas kernels for 0% -> 0%
where the time goes in v1:
time: 69.2 us; the launch traced here: 68.8 us
  Pallas kernels  53.5 us (77%)
  local copies, waits for them, and re-layouts  14.5 us (21%)
    pallas_call x1, Pallas kernels, per_device(): pl.pallas_call(functools.partial(kernel, nseq, nchan, group, scale), out_...  53.5 us
    unnamed x25, local copies, waits for them, and re-layouts  12.1 us

profile of v1, /device:TPU:16, one launch (start us, length us, event | category | flops | bytes accessed | tf_op | source)
XLA Modules:
  0.0 68.8 jit_solution(1947967691392069767)
XLA Ops:
  0.6 0.0 copy-start.9
  0.6 0.7 %copy.22 = f32[1,8]{0,1:T(8,128)S(1)} copy(f32[1,8]{1,0:T(1,128)} %bitcast.11) | data formatting | bytes 64 | tf_op jit(solution)/shard_map/reshape | solution.py:372
  1.4 0.0 copy-done.9
  1.4 0.1 copy.21
  1.5 0.1 maximum_bitcast_fusion
  1.6 0.0 copy-start
  1.6 1.0 %copy-done = f32[2,256,256]{2,1,0:T(8,128)S(1)} copy-done((f32[2,256,256]{2,1,0:T(8,128)S(1)}, f32[2,256,256]{2,1,0:T(8,128)}, u32[]{:S(2)}) %copy-start) | copy-done | bytes 524312
  2.6 0.0 copy-start.1
  2.6 1.0 %copy-done.1 = bf16[2,2,256,256]{3,2,1,0:T(8,128)(2,1)S(1)} copy-done((bf16[2,2,256,256]{3,2,1,0:T(8,128)(2,1)S(1)}, bf16[2,2,256,256]{3,2,1,0:T(8,128)(2,1)}, u32[]{:S(2)}) %copy-start.1) | copy-done | bytes 524312
  3.6 0.0 copy-start.2
  3.6 1.0 %copy-done.2 = bf16[2,256,512]{2,1,0:T(8,128)(2,1)S(1)} copy-done((bf16[2,256,512]{2,1,0:T(8,128)(2,1)S(1)}, bf16[2,256,512]{2,1,0:T(8,128)(2,1)}, u32[]{:S(2)}) %copy-start.2) | copy-done | bytes 524312
  4.7 0.0 copy-start.3
  4.7 1.0 %copy-done.3 = bf16[2,512,256]{2,1,0:T(8,128)(2,1)S(1)} copy-done((bf16[2,512,256]{2,1,0:T(8,128)(2,1)S(1)}, bf16[2,512,256]{2,1,0:T(8,128)(2,1)}, u32[]{:S(2)}) %copy-start.3) | copy-done | bytes 524312
  5.7 0.0 copy-start.4
  5.7 0.9 %copy-done.4 = f32[256,256]{1,0:T(8,128)S(1)} copy-done((f32[256,256]{1,0:T(8,128)S(1)}, f32[256,256]{1,0:T(8,128)}, u32[]{:S(2)}) %copy-start.4) | copy-done | bytes 262168
  6.7 0.0 copy-start.5
  6.7 0.9 %copy-done.5 = bf16[256,256]{1,0:T(8,128)(2,1)S(1)} copy-done((bf16[256,256]{1,0:T(8,128)(2,1)S(1)}, bf16[256,256]{1,0:T(8,128)(2,1)}, u32[]{:S(2)}) %copy-start.5) | copy-done | bytes 131096
  7.6 0.0 copy-start.6
  7.6 0.9 %copy-done.6 = bf16[256,256]{1,0:T(8,128)(2,1)S(1)} copy-done((bf16[256,256]{1,0:T(8,128)(2,1)S(1)}, bf16[256,256]{1,0:T(8,128)(2,1)}, u32[]{:S(2)}) %copy-start.6) | copy-done | bytes 131096
  8.5 0.0 copy-start.7
  8.5 0.9 %copy-done.7 = bf16[256,256]{1,0:T(8,128)(2,1)S(1)} copy-done((bf16[256,256]{1,0:T(8,128)(2,1)S(1)}, bf16[256,256]{1,0:T(8,128)(2,1)}, u32[]{:S(2)}) %copy-start.7) | copy-done | bytes 131096
  9.4 0.0 copy-start.8
  9.4 0.9 %copy-done.8 = bf16[256,256]{1,0:T(8,128)(2,1)S(1)} copy-done((bf16[256,256]{1,0:T(8,128)(2,1)S(1)}, bf16[256,256]{1,0:T(8,128)(2,1)}, u32[]{:S(2)}) %copy-start.8) | copy-done | bytes 131096
  10.3 53.5 %hyena.1 = (bf16[256,256]{1,0:T(8,128)(2,1)S(1)}, bf16[256,256]{1,0:T(8,128)(2,1)S(1)}, bf16[256,256]{1,0:T(8,128)(2,1)S(1)}, bf16[256,256]{1,0:T(8,128)(2,1)S(1...) custom-call(bf16[256,256]{1,0:T(8,128)(2,1)S(1)} %copy-done.5, bf16[256,256]{1,0:T(8,128)(2,1)S(1)} %copy-done.6, ...), custom_call_target="tpu_custom_call" | custom-call | tf_op jit(solution)/shard_map/hyena/pallas_call | solution.py:379
  63.8 0.1 copy.23
  63.9 0.1 copy.25
  64.0 0.7 squeeze.3
  64.7 0.1 copy.24
  64.8 0.7 %reshape.38 = f32[3,3,256]{2,1,0:T(4,128)} reshape(f32[9,32,8]{2,1,0:T(8,128)S(1)} %copy.24) | data formatting | bytes 18432 | tf_op jit(solution)/shard_map/reshape | solution.py:425
  65.5 0.7 copy.31
  66.1 0.7 copy.32
  66.8 0.7 copy.33
  67.5 0.7 copy.34
  68.1 0.7 %copy.35 = f32[256,256]{1,0:T(8,128)} copy(f32[256,256]{1,0:T(8,128)S(1)} %get-tuple-element.30) | data formatting | bytes 524288
  (4 shorter events, 0.0 us)
Async XLA Ops:
  0.6 0.7 %copy-start.9 = (f32[3,3,8]{2,1,0:T(4,128)S(1)}, f32[3,3,8]{2,1,0:T(4,128)}, u32[]{:S(2)}) copy-start(f32[3,3,8]{2,1,0:T(4,128)} %param.15) | copy-start | bytes 868
  1.6 1.0 %copy-start = (f32[2,256,256]{2,1,0:T(8,128)S(1)}, f32[2,256,256]{2,1,0:T(8,128)}, u32[]{:S(2)}) copy-start(f32[2,256,256]{2,1,0:T(8,128)} %constant.14.clone.twist_hbm) | copy-start | bytes 1572868
  2.6 1.0 %copy-start.1 = (bf16[2,2,256,256]{3,2,1,0:T(8,128)(2,1)S(1)}, bf16[2,2,256,256]{3,2,1,0:T(8,128)(2,1)}, u32[]{:S(2)}) copy-start(bf16[2,2,256,256]{3,2,1,0:T(8,128)(2,1)} %constant.13.clone.right_hbm) | copy-start | bytes 1572868
  3.6 1.0 %copy-start.2 = (bf16[2,256,512]{2,1,0:T(8,128)(2,1)S(1)}, bf16[2,256,512]{2,1,0:T(8,128)(2,1)}, u32[]{:S(2)}) copy-start(bf16[2,256,512]{2,1,0:T(8,128)(2,1)} %constant.12.clone.back_hbm) | copy-start | bytes 1572868
  4.7 1.0 %copy-start.3 = (bf16[2,512,256]{2,1,0:T(8,128)(2,1)S(1)}, bf16[2,512,256]{2,1,0:T(8,128)(2,1)}, u32[]{:S(2)}) copy-start(bf16[2,512,256]{2,1,0:T(8,128)(2,1)} %constant.11.clone.left_hbm) | copy-start | bytes 1572868
  5.7 0.9 %copy-start.4 = (f32[256,256]{1,0:T(8,128)S(1)}, f32[256,256]{1,0:T(8,128)}, u32[]{:S(2)}) copy-start(f32[256,256]{1,0:T(8,128)} %h_ref.1) | copy-start | bytes 786436
  6.7 0.9 %copy-start.5 = (bf16[256,256]{1,0:T(8,128)(2,1)S(1)}, bf16[256,256]{1,0:T(8,128)(2,1)}, u32[]{:S(2)}) copy-start(bf16[256,256]{1,0:T(8,128)(2,1)} %q_ref.1) | copy-start | bytes 393220
  7.6 0.9 %copy-start.6 = (bf16[256,256]{1,0:T(8,128)(2,1)S(1)}, bf16[256,256]{1,0:T(8,128)(2,1)}, u32[]{:S(2)}) copy-start(bf16[256,256]{1,0:T(8,128)(2,1)} %k_ref.1) | copy-start | bytes 393220
  8.5 0.9 %copy-start.7 = (bf16[256,256]{1,0:T(8,128)(2,1)S(1)}, bf16[256,256]{1,0:T(8,128)(2,1)}, u32[]{:S(2)}) copy-start(bf16[256,256]{1,0:T(8,128)(2,1)} %v_ref.1) | copy-start | bytes 393220
  9.4 0.9 %copy-start.8 = (bf16[256,256]{1,0:T(8,128)(2,1)S(1)}, bf16[256,256]{1,0:T(8,128)(2,1)}, u32[]{:S(2)}) copy-start(bf16[256,256]{1,0:T(8,128)(2,1)} %c_ref.1) | copy-start | bytes 393220

commit v2 on v1

--- a/solution.py
+++ b/solution.py
@@ -77,22 +77,30 @@
     nchan,
     group,
     scale,
+    q_hbm,
+    k_hbm,
+    v_hbm,
+    c_hbm,
+    h_hbm,
+    taps_hbm,
+    gain_hbm,
+    left_hbm,
+    back_hbm,
+    right_hbm,
+    twist_hbm,
+    go_hbm,
+    qg_hbm,
+    kg_hbm,
+    vg_hbm,
+    fg_hbm,
+    sums_hbm,
     q_ref,
     k_ref,
     v_ref,
     c_ref,
     h_ref,
-    side_ref,
-    left_hbm,
-    back_hbm,
-    right_hbm,
-    twist_hbm,
-    go_ref,
-    qg_ref,
-    kg_ref,
-    vg_ref,
-    fg_ref,
-    sums_ref,
+    taps_own,
+    gain_own,
     left,
     back,
     right,
@@ -103,7 +111,8 @@
     got_h,
     got_kv,
     got_qc,
-    side,
+    taps_ref,
+    gain_ref,
     out_gq,
     out_f,
     out_kv,
@@ -124,6 +133,13 @@
     spec_h,
     spec_p,
     spec_g,
+    go_ref,
+    qg_ref,
+    kg_ref,
+    vg_ref,
+    fg_ref,
+    input_sem,
+    out_sem,
     table_sem,
     send_sem,
     recv_sem,
@@ -131,15 +147,29 @@
 ):
     me = lax.axis_index("seq")
     mine = lax.axis_index("chan")
-    rows, width = q_ref.shape
-
+    rows, width = q_hbm.shape
+
+    inputs = [
+        pltpu.make_async_copy(src, dst, input_sem.at[i])
+        for i, (src, dst) in enumerate(
+            [
+                (h_hbm, h_ref),
+                (k_hbm, k_ref),
+                (v_hbm, v_ref),
+                (q_hbm, q_ref),
+                (c_hbm, c_ref),
+                (taps_hbm, taps_own),
+                (gain_hbm, gain_own),
+            ]
+        )
+    ]
     tables = [
         pltpu.make_async_copy(src, dst, table_sem.at[i])
         for i, (src, dst) in enumerate(
-            [(left_hbm, left), (back_hbm, back), (right_hbm, right), (twist_hbm, twist)]
+            [(left_hbm, left), (twist_hbm, twist), (right_hbm, right), (back_hbm, back)]
         )
     ]
-    for copy in tables:
+    for copy in inputs + tables:
         copy.start()
 
     per = nseq // nchan
@@ -164,6 +194,7 @@
             barrier, inc=1, device_id=(from_seq, from_chan), device_id_type=MESH
         )
 
+    inputs[0].wait()
     send_h[...] = h_ref[...].T.reshape(nseq, group, width)
 
     @pl.when(stays)
@@ -202,22 +233,29 @@
 
     send_all(send_h, got_h, 0)
 
-    side_copy = pltpu.make_async_remote_copy(
-        src_ref=side_ref,
-        dst_ref=side,
-        send_sem=side_sem.at[0],
-        recv_sem=side_sem.at[1],
-        device_id=(to_seq, to_chan),
-        device_id_type=MESH,
-    )
+    side_copies = [
+        pltpu.make_async_remote_copy(
+            src_ref=src,
+            dst_ref=dst,
+            send_sem=side_sem.at[i],
+            recv_sem=side_sem.at[2 + i],
+            device_id=(to_seq, to_chan),
+            device_id_type=MESH,
+        )
+        for i, (src, dst) in enumerate([(taps_own, taps_ref), (gain_own, gain_ref)])
+    ]
+    inputs[5].wait()
+    inputs[6].wait()
 
     @pl.when(jnp.logical_not(stays))
     def _():
-        side_copy.start()
+        for copy in side_copies:
+            copy.start()
 
     @pl.when(stays)
     def _():
-        side[...] = side_ref[...]
+        taps_ref[...] = taps_own[...]
+        gain_ref[...] = gain_own[...]
 
     def paired(first, second):
         shape = (nseq, group, width)
@@ -225,8 +263,12 @@
         two = second[...].astype(F32).T.reshape(shape)
         return jnp.concatenate([one, two], axis=1).astype(BF16)
 
+    inputs[1].wait()
+    inputs[2].wait()
     send_kv[...] = paired(k_ref, v_ref)
     send_all(send_kv, got_kv, 1)
+    inputs[3].wait()
+    inputs[4].wait()
     send_qc[...] = paired(q_ref, c_ref)
     send_all(send_qc, got_qc, 2)
 
@@ -263,10 +305,19 @@
 
     @pl.when(jnp.logical_not(stays))
     def _():
-        side_copy.wait()
-
-    taps = [[side[:, 3 * s + i : 3 * s + i + 1] for i in range(3)] for s in range(3)]
-    gain = side[:, 9:10]
+        for copy in side_copies:
+            copy.wait()
+
+    diagonal = lax.broadcasted_iota(jnp.int32, (group, group), 0) == lax.broadcasted_iota(
+        jnp.int32, (group, group), 1
+    )
+
+    def column(row):
+        spread_out = jnp.broadcast_to(row, (group, group))
+        return jnp.sum(jnp.where(diagonal, spread_out, 0.0), axis=1, keepdims=True)
+
+    taps = [[column(taps_ref[s, i : i + 1, :]) for i in range(3)] for s in range(3)]
+    gain = column(gain_ref[...])
 
     def short(value, keep, coeffs):
         one, two = delayed(value, 1), delayed(value, 2)
@@ -350,17 +401,67 @@
         first[...] = both[:, :group].reshape(rows, width).T.astype(BF16)
         second[...] = both[:, group:].reshape(rows, width).T.astype(BF16)
 
+    writes = [
+        pltpu.make_async_copy(src, dst, out_sem.at[i])
+        for i, (src, dst) in enumerate(
+            [
+                (go_ref, go_hbm),
+                (qg_ref, qg_hbm),
+                (fg_ref, fg_hbm),
+                (kg_ref, kg_hbm),
+                (vg_ref, vg_hbm),
+                (in_s, sums_hbm),
+            ]
+        )
+    ]
     arrived(in_gq, 3)
     unpaired(in_gq, go_ref, qg_ref)
+    writes[0].start()
+    writes[1].start()
     arrived(in_f, 4)
     fg_ref[...] = in_f[...].reshape(rows, width).T
+    writes[2].start()
     arrived(in_kv, 5)
     unpaired(in_kv, kg_ref, vg_ref)
+    writes[3].start()
+    writes[4].start()
     arrived(in_s, 6)
-    sums_ref[...] = in_s[...]
+    writes[5].start()
+    for copy in writes:
+        copy.wait()
 
     for index, source in enumerate([send_h, send_kv, send_qc, out_gq, out_f, out_kv, out_s]):
         sent(source, index)
+
+
+def deliver(go, qg, kg, vg, fg, sums, go_out, qg_out, kg_out, vg_out, fg_out, taps_out, gain_out, held, sem):
+    nseq, group = sums.shape[0], gain_out.shape[1] // sums.shape[0]
+    pairs = [(sums, held), (go, go_out), (qg, qg_out), (kg, kg_out), (vg, vg_out), (fg, fg_out)]
+    copies = [pltpu.make_async_copy(src, dst, sem.at[i]) for i, (src, dst) in enumerate(pairs)]
+    for copy in copies:
+        copy.start()
+    copies[0].wait()
+    table = held[...].reshape(nseq, 128)
+    turned = jnp.concatenate(
+        [table if r == 0 else pltpu.roll(table, 128 - group * r, 1) for r in range(10)], axis=0
+    )
+    width = gain_out.shape[1]
+    channel = lax.broadcasted_iota(jnp.int32, (128, width), 1)
+    pick = lax.rem(channel, group) == lax.broadcasted_iota(jnp.int32, (128, width), 0)
+    wide = jnp.dot(
+        turned,
+        pick.astype(F32),
+        preferred_element_type=F32,
+        precision=lax.Precision.HIGHEST,
+    ).reshape(10, nseq, width)
+    owner = lax.div(lax.broadcasted_iota(jnp.int32, (nseq, width), 1), group)
+    keep = owner == lax.broadcasted_iota(jnp.int32, (nseq, width), 0)
+    rows = [jnp.sum(jnp.where(keep, wide[r], 0.0), axis=0, keepdims=True) for r in range(10)]
+    for r in range(9):
+        taps_out[r // 3, r % 3 : r % 3 + 1, :] = rows[r]
+    gain_out[...] = rows[9]
+    for copy in copies[1:]:
+        copy.wait()
 
 
 def per_device(query_rows, key_rows, value_rows, long_filter, short_taps, skip_gain, cotangent):
@@ -369,11 +470,9 @@
     group = channels // nseq
     scale = 1.0 / math.sqrt(rows * nseq)
     tables = [jnp.asarray(t) for t in transform_tables(nseq, rows, group)]
-    side = jnp.concatenate([short_taps.reshape(9, group), skip_gain.reshape(1, group)], axis=0)
-    side = jnp.pad(side.T, ((0, 0), (0, 128 - 10)))
     block = jax.ShapeDtypeStruct((rows, channels), BF16)
     vmem = pl.BlockSpec(memory_space=pltpu.VMEM)
-    hbm = pl.BlockSpec(memory_space=pl.ANY)
+    hbm = pl.BlockSpec(memory_space=pltpu.HBM)
     one, two = (nseq, group, rows), (nseq, 2 * group, rows)
     spec = pltpu.VMEM((2, nseq * group, rows), F32)
     outs = pl.pallas_call(
@@ -386,9 +485,15 @@
             jax.ShapeDtypeStruct((rows, channels), F32),
             jax.ShapeDtypeStruct((nseq, 1, 128), F32),
         ),
-        in_specs=[vmem] * 6 + [hbm] * 4,
-        out_specs=[vmem] * 6,
-        scratch_shapes=[pltpu.VMEM(t.shape, t.dtype) for t in tables]
+        in_specs=[hbm] * 11,
+        out_specs=[hbm] * 6,
+        scratch_shapes=[pltpu.VMEM((rows, channels), BF16)] * 4
+        + [
+            pltpu.VMEM((rows, channels), F32),
+            pltpu.VMEM((3, 3, group), F32),
+            pltpu.VMEM((1, group), F32),
+        ]
+        + [pltpu.VMEM(t.shape, t.dtype) for t in tables]
         + [
             pltpu.VMEM(one, F32),
             pltpu.VMEM(two, BF16),
@@ -396,7 +501,8 @@
             pltpu.VMEM(one, F32),
             pltpu.VMEM(two, BF16),
             pltpu.VMEM(two, BF16),
-            pltpu.VMEM((group, 128), F32),
+            pltpu.VMEM((3, 3, group), F32),
+            pltpu.VMEM((1, group), F32),
             pltpu.VMEM(two, BF16),
             pltpu.VMEM(one, F32),
             pltpu.VMEM(two, BF16),
@@ -409,20 +515,34 @@
         + [pltpu.VMEM(one, F32)] * 6
         + [pltpu.VMEM((2,) + one, F32)] * 3
         + [spec] * 3
+        + [pltpu.VMEM((rows, channels), BF16)] * 4
+        + [pltpu.VMEM((rows, channels), F32)]
         + [
+            pltpu.SemaphoreType.DMA((7,)),
+            pltpu.SemaphoreType.DMA((6,)),
             pltpu.SemaphoreType.DMA((4,)),
             pltpu.SemaphoreType.DMA((7,)),
             pltpu.SemaphoreType.DMA((7,)),
-            pltpu.SemaphoreType.DMA((2,)),
+            pltpu.SemaphoreType.DMA((4,)),
         ],
         compiler_params=pltpu.CompilerParams(
-            collective_id=0, has_side_effects=True, vmem_limit_bytes=48 << 20
+            collective_id=0, has_side_effects=True, vmem_limit_bytes=60 << 20
         ),
         name="hyena",
-    )(query_rows, key_rows, value_rows, cotangent, long_filter, side, *tables)
-    sums = outs[5].reshape(nseq, 128)[:, : 10 * group].reshape(nseq, 10, group)
-    sums = sums.transpose(1, 0, 2).reshape(10, channels)
-    return outs[:5] + (sums[:9].reshape(3, 3, channels), sums[9])
+    )(query_rows, key_rows, value_rows, cotangent, long_filter, short_taps, skip_gain[None], *tables)
+    moved = pl.pallas_call(
+        deliver,
+        out_shape=tuple(jax.ShapeDtypeStruct(o.shape, o.dtype) for o in outs[:5])
+        + (
+            jax.ShapeDtypeStruct((3, 3, channels), F32),
+            jax.ShapeDtypeStruct((1, channels), F32),
+        ),
+        in_specs=[hbm] * 6,
+        out_specs=[hbm] * 5 + [vmem] * 2,
+        scratch_shapes=[pltpu.VMEM((nseq, 1, 128), F32), pltpu.SemaphoreType.DMA((6,))],
+        name="deliver",
+    )(*outs)
+    return tuple(moved[:6]) + (moved[6].reshape(channels),)
 
 
 def solution(mesh):

time: 69.2 us -> 80.7 us (1.17)
  Pallas kernels: 53.5 us -> 79.8 us
  local copies, waits for them, and re-layouts: 14.5 us -> 0 us
    pallas_call x0 -> x1, Pallas kernels: none -> 25.6 us  [per_device(): pl.pallas_call(deliver, out_shape=tuple((jax.ShapeDtypeStruct(o.shape, o....]
    unnamed x25 -> x0, local copies, waits for them, and re-layouts: 12.1 us -> none
    reshape x4 -> x0, local copies, waits for them, and re-layouts: 1.56 us -> none  [the longest x1 0.74 us: per_device(): skip_gain.reshape(1, group)]
where the time goes in v2:
time: 80.7 us; the launch traced here: 80.5 us
  Pallas kernels  79.8 us (99%)
    pallas_call x1, Pallas kernels, per_device(): pl.pallas_call(functools.partial(kernel, nseq, nchan, group, scale), out_...  54.2 us
    pallas_call x1, Pallas kernels, per_device(): pl.pallas_call(deliver, out_shape=tuple((jax.ShapeDtypeStruct(o.shape, o....  25.6 us

profile of v2, /device:TPU:16, one launch (start us, length us, event | category | flops | bytes accessed | tf_op | source)
XLA Modules:
  0.0 80.5 jit_solution(8171606566720605915)
XLA Ops:
  0.6 54.2 %hyena.1 = (bf16[256,256]{1,0:T(8,128)(2,1)}, bf16[256,256]{1,0:T(8,128)(2,1)}, bf16[256,256]{1,0:T(8,128)(2,1)}, bf16[256,256]{1,0:T(8,128)(2,1)}, f32[256,256]{1,0:T(8,128)}, /*index=5*/f32[32,1,128]{2,1,0:T(1,128)}) custom-call(bf16[256,256]{1,0:T(8,128)(2,1)} %q_hbm.1, bf16[256,256]{1,0:T(8,128)(2,1)} %k_hbm.1, bf16[256,256]{1,0:T(8,128)(2,1)} %v_hbm.1, ...), custom_call_target="tpu_custom_call" | custom-call | tf_op jit(solution)/shard_map/hyena/pallas_call | solution.py:478
  54.9 25.6 %deliver.1 = (bf16[256,256]{1,0:T(8,128)(2,1)}, bf16[256,256]{1,0:T(8,128)(2,1)}, bf16[256,256]{1,0:T(8,128)(2,1)}, bf16[256,256]{1,0:T(8,128)(2,1)}, f32[256,25...) custom-call(bf16[256,256]{1,0:T(8,128)(2,1)} %get-tuple-element.20.go, bf16[256,256]{1,0:T(8,128)(2,1)} %get-tuple-element.21.qg, ...), custom_call_target="tpu_custom_call" | custom-call | tf_op jit(solution)/shard_map/deliver/pallas_call | solution.py:533

commit v3 on v2

--- a/solution.py
+++ b/solution.py
@@ -88,12 +88,12 @@
     back_hbm,
     right_hbm,
     twist_hbm,
-    go_hbm,
-    qg_hbm,
-    kg_hbm,
-    vg_hbm,
-    fg_hbm,
-    sums_hbm,
+    go_ref,
+    qg_ref,
+    kg_ref,
+    vg_ref,
+    fg_ref,
+    sums_ref,
     q_ref,
     k_ref,
     v_ref,
@@ -133,13 +133,7 @@
     spec_h,
     spec_p,
     spec_g,
-    go_ref,
-    qg_ref,
-    kg_ref,
-    vg_ref,
-    fg_ref,
     input_sem,
-    out_sem,
     table_sem,
     send_sem,
     recv_sem,
@@ -401,47 +395,25 @@
         first[...] = both[:, :group].reshape(rows, width).T.astype(BF16)
         second[...] = both[:, group:].reshape(rows, width).T.astype(BF16)
 
-    writes = [
-        pltpu.make_async_copy(src, dst, out_sem.at[i])
-        for i, (src, dst) in enumerate(
-            [
-                (go_ref, go_hbm),
-                (qg_ref, qg_hbm),
-                (fg_ref, fg_hbm),
-                (kg_ref, kg_hbm),
-                (vg_ref, vg_hbm),
-                (in_s, sums_hbm),
-            ]
-        )
-    ]
     arrived(in_gq, 3)
     unpaired(in_gq, go_ref, qg_ref)
-    writes[0].start()
-    writes[1].start()
     arrived(in_f, 4)
     fg_ref[...] = in_f[...].reshape(rows, width).T
-    writes[2].start()
     arrived(in_kv, 5)
     unpaired(in_kv, kg_ref, vg_ref)
-    writes[3].start()
-    writes[4].start()
     arrived(in_s, 6)
-    writes[5].start()
-    for copy in writes:
-        copy.wait()
-
+    sums_ref[...] = in_s[...]
     for index, source in enumerate([send_h, send_kv, send_qc, out_gq, out_f, out_kv, out_s]):
         sent(source, index)
 
 
-def deliver(go, qg, kg, vg, fg, sums, go_out, qg_out, kg_out, vg_out, fg_out, taps_out, gain_out, held, sem):
+def deliver(go, qg, kg, vg, fg, sums, go_out, qg_out, kg_out, vg_out, fg_out, taps_out, gain_out, sem):
     nseq, group = sums.shape[0], gain_out.shape[1] // sums.shape[0]
-    pairs = [(sums, held), (go, go_out), (qg, qg_out), (kg, kg_out), (vg, vg_out), (fg, fg_out)]
+    pairs = [(go, go_out), (qg, qg_out), (kg, kg_out), (vg, vg_out), (fg, fg_out)]
     copies = [pltpu.make_async_copy(src, dst, sem.at[i]) for i, (src, dst) in enumerate(pairs)]
     for copy in copies:
         copy.start()
-    copies[0].wait()
-    table = held[...].reshape(nseq, 128)
+    table = sums[...].reshape(nseq, 128)
     turned = jnp.concatenate(
         [table if r == 0 else pltpu.roll(table, 128 - group * r, 1) for r in range(10)], axis=0
     )
@@ -460,7 +432,7 @@
     for r in range(9):
         taps_out[r // 3, r % 3 : r % 3 + 1, :] = rows[r]
     gain_out[...] = rows[9]
-    for copy in copies[1:]:
+    for copy in copies:
         copy.wait()
 
 
@@ -486,7 +458,7 @@
             jax.ShapeDtypeStruct((nseq, 1, 128), F32),
         ),
         in_specs=[hbm] * 11,
-        out_specs=[hbm] * 6,
+        out_specs=[vmem] * 6,
         scratch_shapes=[pltpu.VMEM((rows, channels), BF16)] * 4
         + [
             pltpu.VMEM((rows, channels), F32),
@@ -515,21 +487,26 @@
         + [pltpu.VMEM(one, F32)] * 6
         + [pltpu.VMEM((2,) + one, F32)] * 3
         + [spec] * 3
-        + [pltpu.VMEM((rows, channels), BF16)] * 4
-        + [pltpu.VMEM((rows, channels), F32)]
         + [
             pltpu.SemaphoreType.DMA((7,)),
-            pltpu.SemaphoreType.DMA((6,)),
             pltpu.SemaphoreType.DMA((4,)),
             pltpu.SemaphoreType.DMA((7,)),
             pltpu.SemaphoreType.DMA((7,)),
             pltpu.SemaphoreType.DMA((4,)),
         ],
         compiler_params=pltpu.CompilerParams(
-            collective_id=0, has_side_effects=True, vmem_limit_bytes=60 << 20
+            collective_id=0, has_side_effects=True, vmem_limit_bytes=40 << 20
         ),
         name="hyena",
-    )(query_rows, key_rows, value_rows, cotangent, long_filter, short_taps, skip_gain[None], *tables)
+    )(
+        *[
+            pltpu.with_memory_space_constraint(x, pltpu.HBM)
+            for x in (
+                query_rows, key_rows, value_rows, cotangent, long_filter, short_taps,
+                skip_gain[None], *tables,
+            )
+        ]
+    )
     moved = pl.pallas_call(
         deliver,
         out_shape=tuple(jax.ShapeDtypeStruct(o.shape, o.dtype) for o in outs[:5])
@@ -537,9 +514,10 @@
             jax.ShapeDtypeStruct((3, 3, channels), F32),
             jax.ShapeDtypeStruct((1, channels), F32),
         ),
-        in_specs=[hbm] * 6,
+        in_specs=[vmem] * 6,
         out_specs=[hbm] * 5 + [vmem] * 2,
-        scratch_shapes=[pltpu.VMEM((nseq, 1, 128), F32), pltpu.SemaphoreType.DMA((6,))],
+        scratch_shapes=[pltpu.SemaphoreType.DMA((5,))],
+        compiler_params=pltpu.CompilerParams(vmem_limit_bytes=16 << 20),
         name="deliver",
     )(*outs)
     return tuple(moved[:6]) + (moved[6].reshape(channels),)

time: 80.7 us -> 55.9 us (0.69)
  Pallas kernels: 79.8 us -> 55.1 us
    pallas_call x1, Pallas kernels: 25.6 us -> 1.53 us  [per_device(): pl.pallas_call(deliver, out_shape=tuple((jax.ShapeDtypeStruct(o.shape, o....]
where the time goes in v3:
time: 55.9 us; the launch traced here: 55.8 us
  Pallas kernels  55.1 us (99%)
  between operations  0.64 us (1%)
    pallas_call x1, Pallas kernels, per_device(): pl.pallas_call(functools.partial(kernel, nseq, nchan, group, scale), out_...  53.6 us
    pallas_call x1, Pallas kernels, per_device(): pl.pallas_call(deliver, out_shape=tuple((jax.ShapeDtypeStruct(o.shape, o....  1.53 us

profile of v3, /device:TPU:16, one launch (start us, length us, event | category | flops | bytes accessed | tf_op | source)
XLA Modules:
  0.0 55.8 jit_solution(5845881777665001786)
XLA Ops:
  0.6 53.6 %hyena.1 = (bf16[256,256]{1,0:T(8,128)(2,1)S(1)}, bf16[256,256]{1,0:T(8,128)(2,1)S(1)}, bf16[256,256]{1,0:T(8,128)(2,1)S(1)}, bf16[256,256]{1,0:T(8,128)(2,1)S(1...) custom-call(bf16[256,256]{1,0:T(8,128)(2,1)} %q_hbm.1, bf16[256,256]{1,0:T(8,128)(2,1)} %k_hbm.1, ...), custom_call_target="tpu_custom_call" | custom-call | tf_op jit(solution)/shard_map/hyena/pallas_call | solution.py:450
  54.2 1.5 %deliver.1 = (bf16[256,256]{1,0:T(8,128)(2,1)}, bf16[256,256]{1,0:T(8,128)(2,1)}, bf16[256,256]{1,0:T(8,128)(2,1)}, bf16[256,256]{1,0:T(8,128)(2,1)}, f32[256,25...) custom-call(bf16[256,256]{1,0:T(8,128)(2,1)S(1)} %get-tuple-element.20.go, ...), custom_call_target="tpu_custom_call" | custom-call | tf_op jit(solution)/shard_map/deliver/pallas_call | solution.py:510

commit v4 on v1

v4 whole, which is shorter than its diff:
```python
import functools
import math
import types

import jax
import jax.numpy as jnp
import ml_dtypes
import numpy as np
from jax import lax
from jax.experimental import pallas as pl
from jax.experimental.pallas import tpu as pltpu
from jax.sharding import PartitionSpec as P

F32 = jnp.float32
BF16 = jnp.bfloat16
MESH = pl.DeviceIdType.MESH
REACH = 125.0 * math.log(2.0)


def halves(table):
    high = table.astype(np.float32).astype(ml_dtypes.bfloat16)
    low = (table - high.astype(np.float64)).astype(np.float32).astype(ml_dtypes.bfloat16)
    return np.stack([high, low])


def transform_tables(blocks, width, group):
    total = blocks * width
    shifted = np.arange(blocks) - 0.25
    outer = 2.0 * np.pi / blocks * np.outer(shifted, np.arange(blocks))
    eye = np.eye(group)
    left = np.concatenate([np.kron(np.cos(outer), eye), np.kron(-np.sin(outer), eye)], axis=0)
    back = left.T / total
    inner = 2.0 * np.pi / width * (np.outer(np.arange(width), np.arange(width)) % width)
    right = np.stack([halves(np.cos(inner)), halves(np.sin(inner))])
    turn = 2.0 * np.pi / total * np.outer(shifted, np.arange(width))
    twist = np.stack([np.cos(turn), np.sin(turn)]).astype(np.float32)
    twist = np.repeat(twist, group, axis=1)
    return halves(left), halves(back), right, twist


def split(value):
    high = value.astype(BF16)
    return high, (value - high.astype(F32)).astype(BF16)


def dot(left, right):
    return jnp.dot(left, right, preferred_element_type=F32)


def dot3(left, right):
    return dot(left[0], right[0]) + dot(left[0], right[1]) + dot(left[1], right[0])


def delayed(value, steps):
    before = jnp.concatenate([jnp.zeros_like(value[:1]), value[:-1]], axis=0)
    lane = lax.broadcasted_iota(jnp.int32, value.shape, 2)
    return jnp.where(
        lane < steps, pltpu.roll(before, steps, 2), pltpu.roll(value, steps, 2)
    )


def later(value, head, steps):
    return pltpu.roll(jnp.concatenate([head, value], axis=0), steps, 0)[head.shape[0] :]


def block_ends(grad, coeffs):
    half = grad.shape[2] // 2
    low, high = grad[:, :, :half], grad[:, :, half:]
    after = jnp.concatenate([low[1:], jnp.zeros_like(low[:1])], axis=0)
    lane = lax.broadcasted_iota(jnp.int32, high.shape, 2)
    total = coeffs[0] * high
    for steps in (1, 2):
        moved = jnp.where(
            lane < half - steps,
            pltpu.roll(high, half - steps, 2),
            pltpu.roll(after, half - steps, 2),
        )
        total = total + coeffs[steps] * moved
    return [
        jnp.sum(jnp.where(lane == half - back, total, 0.0), axis=2, keepdims=True)
        for back in (2, 1)
    ]


def total_of(value):
    return jnp.sum(jnp.sum(value, axis=0), axis=1, keepdims=True)


def encode(value):
    peak = jnp.maximum(jnp.max(jnp.abs(value), axis=2, keepdims=True), 1e-30)
    code = jnp.exp(jnp.abs(value) * (2.0 * REACH / peak) - REACH)
    code = jnp.where(value < 0.0, -code, code)
    half = value.shape[2] // 2
    return jnp.concatenate([code[:, :, :half], code[:, :, half:]], axis=1).astype(BF16), peak


def decode(code, peak):
    group = code.shape[1] // 2
    code = code.astype(F32)
    code = jnp.concatenate([code[:, :group], code[:, group:]], axis=2)
    size = (jnp.log(jnp.abs(code)) + REACH) * (peak * (0.5 / REACH))
    return jnp.where(code < 0.0, -size, size)


def field_mask(group, field):
    lane = lax.broadcasted_iota(jnp.int32, (1, group, 128), 2)
    return lane == group * field + lax.broadcasted_iota(jnp.int32, (1, group, 128), 1)


def packed_rows(count, group, fields):
    wide = jnp.zeros((count, group, 128), F32)
    for field, value in fields.items():
        wide = jnp.where(field_mask(group, field), value, wide)
    return jnp.sum(wide, axis=1, keepdims=True)


def unpacked(rows, group, field):
    wide = jnp.broadcast_to(rows, (rows.shape[0], group, 128))
    return jnp.sum(jnp.where(field_mask(group, field), wide, 0.0), axis=2, keepdims=True)


def channel_rows(table, count, group):
    owners = table.shape[0]
    width = owners * group
    turned = jnp.concatenate(
        [table if f == 0 else pltpu.roll(table, 128 - group * f, 1) for f in range(count)],
        axis=0,
    )
    channel = lax.broadcasted_iota(jnp.int32, (128, width), 1)
    pick = lax.rem(channel, group) == lax.broadcasted_iota(jnp.int32, (128, width), 0)
    wide = jnp.dot(
        turned,
        pick.astype(F32),
        preferred_element_type=F32,
        precision=lax.Precision.HIGHEST,
    ).reshape(count, owners, width)
    owner = lax.div(lax.broadcasted_iota(jnp.int32, (owners, width), 1), group)
    keep = owner == lax.broadcasted_iota(jnp.int32, (owners, width), 0)
    return [jnp.sum(jnp.where(keep, wide[f], 0.0), axis=0, keepdims=True) for f in range(count)]


HALO = 16
MESSAGES = ("kv", "h", "hs", "qc", "t", "m", "ms", "p", "ps", "f", "fs", "s")


def kernel(names, nseq, nchan, group, scale, *refs):
    r = types.SimpleNamespace(**dict(zip(names, refs, strict=True)))
    me = lax.axis_index("seq")
    mine = lax.axis_index("chan")
    rows, width = r.q_hbm.shape
    number = {name: i for i, name in enumerate(MESSAGES)}

    fetched = {}
    pairs = [("k", "k"), ("v", "v"), ("h", "h"), ("q", "q"), ("c", "c"), ("taps", "taps_own")]
    pairs += [("gain", "gain_own"), ("left", "left"), ("twist", "twist")]
    pairs += [("right", "right"), ("back", "back")]
    for i, (src, dst) in enumerate(pairs):
        fetched[src] = pltpu.make_async_copy(
            getattr(r, src + "_hbm"), getattr(r, dst), r.fetch_sem.at[i]
        )
        fetched[src].start()

    per = nseq // nchan
    to_seq = nchan * lax.rem(me, per) + mine
    to_chan = lax.div(me, per)
    from_seq = per * mine + lax.div(me, nchan)
    from_chan = lax.rem(me, nchan)
    stays = jnp.logical_and(to_seq == me, to_chan == mine)

    barrier = pltpu.get_barrier_semaphore()

    def greet(step, carry):
        peer = lax.rem(me + step, nseq)
        pl.semaphore_signal(barrier, inc=1, device_id=(peer, mine), device_id_type=MESH)
        return carry

    lax.fori_loop(1, nseq, greet, 0)

    @pl.when(jnp.logical_not(stays))
    def _():
        pl.semaphore_signal(
            barrier, inc=1, device_id=(from_seq, from_chan), device_id_type=MESH
        )

    shape = (nseq, group, width)

    def paired(first, second):
        one = first[...].astype(F32).T.reshape(shape)
        two = second[...].astype(F32).T.reshape(shape)
        return jnp.concatenate([one, two], axis=1).astype(BF16)

    fetched["k"].wait()
    fetched["v"].wait()
    r.send_kv[...] = paired(r.k, r.v)

    @pl.when(stays)
    def _():
        pl.semaphore_wait(barrier, nseq - 1)

    @pl.when(jnp.logical_not(stays))
    def _():
        pl.semaphore_wait(barrier, nseq)

    def send_all(name):
        source, target = getattr(r, "send_" + name), getattr(r, "got_" + name)
        index = number[name]

        def body(step, carry):
            peer = lax.rem(me + step, nseq)
            pltpu.make_async_remote_copy(
                src_ref=source.at[peer],
                dst_ref=target.at[me],
                send_sem=r.send_sem.at[index],
                recv_sem=r.recv_sem.at[index],
                device_id=(peer, mine),
                device_id_type=MESH,
            ).start()
            return carry

        lax.fori_loop(1, nseq, body, 0)
        target[me] = source[me]

    def arrived(name):
        part = getattr(r, "got_" + name).at[pl.ds(0, nseq - 1)]
        pltpu.make_async_copy(part, part, r.recv_sem.at[number[name]]).wait()

    def sent(name):
        part = getattr(r, "send_" + name).at[pl.ds(0, nseq - 1)]
        pltpu.make_async_copy(part, part, r.send_sem.at[number[name]]).wait()

    send_all("kv")

    side_copies = [
        pltpu.make_async_remote_copy(
            src_ref=src,
            dst_ref=dst,
            send_sem=r.side_sem.at[i],
            recv_sem=r.side_sem.at[2 + i],
            device_id=(to_seq, to_chan),
            device_id_type=MESH,
        )
        for i, (src, dst) in enumerate([(r.taps_own, r.taps), (r.gain_own, r.gain)])
    ]
    fetched["taps"].wait()
    fetched["gain"].wait()

    @pl.when(jnp.logical_not(stays))
    def _():
        for copy in side_copies:
            copy.start()

    @pl.when(stays)
    def _():
        r.taps[...] = r.taps_own[...]
        r.gain[...] = r.gain_own[...]

    fetched["h"].wait()
    r.send_h[...], peak = encode(r.h[...].T.reshape(shape))
    r.send_hs[...] = packed_rows(nseq, group, {0: peak})
    send_all("h")
    send_all("hs")

    fetched["q"].wait()
    fetched["c"].wait()
    r.send_qc[...] = paired(r.q, r.c)
    send_all("qc")

    halo_copies = [
        pltpu.make_async_remote_copy(
            src_ref=src.at[pl.ds(rows - HALO, HALO)],
            dst_ref=r.halo.at[i],
            send_sem=r.halo_sem.at[i],
            recv_sem=r.halo_sem.at[3 + i],
            device_id=(lax.rem(me + 1, nseq), mine),
            device_id_type=MESH,
        )
        for i, src in enumerate([r.q, r.k, r.v])
    ]

    @pl.when(me < nseq - 1)
    def _():
        for copy in halo_copies:
            copy.start()

    @pl.when(me == 0)
    def _():
        r.halo[...] = jnp.zeros(r.halo.shape, BF16)

    @pl.when(jnp.logical_not(stays))
    def _():
        for copy in side_copies:
            copy.wait()

    diagonal = field_mask(group, 0)[0, :, :group]

    def column(row):
        spread_out = jnp.broadcast_to(row, (group, group))
        return jnp.sum(jnp.where(diagonal, spread_out, 0.0), axis=1, keepdims=True)

    taps = [[column(r.taps[s, i : i + 1, :]) for i in range(3)] for s in range(3)]
    gain = column(r.gain[...])
    r.send_t[...] = jnp.broadcast_to(
        packed_rows(1, group, {3 * s + i: taps[s][i] for s in range(3) for i in range(3)}),
        r.send_t.shape,
    )
    send_all("t")

    for name in ("left", "twist", "right", "back"):
        fetched[name].wait()

    def forward(signal, spec):
        parts = split(signal.reshape(rows, width))
        wave = dot3((r.left[0], r.left[1]), parts)
        real, imag = wave[:rows], wave[rows:]
        cosine, sine = r.twist[0], r.twist[1]
        turned_real = split(real * cosine + imag * sine)
        turned_imag = split(imag * cosine - real * sine)
        cos_parts = (r.right[0, 0], r.right[0, 1])
        sin_parts = (r.right[1, 0], r.right[1, 1])
        spec[0] = dot3(turned_real, cos_parts) + dot3(turned_imag, sin_parts)
        spec[1] = dot3(turned_imag, cos_parts) - dot3(turned_real, sin_parts)

    def inverse(left_spec, right_spec, conjugate):
        a_re, a_im, b_re, b_im = left_spec[0], left_spec[1], right_spec[0], right_spec[1]
        if conjugate:
            real, imag = a_re * b_re + a_im * b_im, a_re * b_im - a_im * b_re
        else:
            real, imag = a_re * b_re - a_im * b_im, a_re * b_im + a_im * b_re
        real, imag = split(real), split(imag)
        cos_parts = (r.right[0, 0], r.right[0, 1])
        sin_parts = (r.right[1, 0], r.right[1, 1])
        wave_real = dot3(real, cos_parts) - dot3(imag, sin_parts)
        wave_imag = dot3(imag, cos_parts) + dot3(real, sin_parts)
        cosine, sine = r.twist[0], r.twist[1]
        turned_real = split(wave_real * cosine - wave_imag * sine)
        turned_imag = split(wave_imag * cosine + wave_real * sine)
        signal = dot3((r.back[0, :, :rows], r.back[1, :, :rows]), turned_real)
        signal = signal + dot3((r.back[0, :, rows:], r.back[1, :, rows:]), turned_imag)
        return signal.reshape(shape)

    def short(value, keep, coeffs):
        one, two = delayed(value, 1), delayed(value, 2)
        keep[0] = one
        keep[1] = two
        return coeffs[0] * value + coeffs[1] * one + coeffs[2] * two

    arrived("kv")
    both = r.got_kv[...].astype(F32)
    r.x_k[...] = both[:, :group]
    r.x_v[...] = both[:, group:]
    r.key_conv[...] = short(r.x_k[...], r.d_k, taps[1])
    r.value_conv[...] = short(r.x_v[...], r.d_v, taps[2])
    r.x_p[...] = r.key_conv[...] * r.value_conv[...]
    forward(r.x_p[...], r.spec_p)

    arrived("h")
    arrived("hs")
    forward(decode(r.got_h[...], unpacked(r.got_hs[...], group, 0)), r.spec_h)
    r.x_m[...] = inverse(r.spec_h, r.spec_p, False) + gain * r.x_p[...]
    r.send_m[...], peak = encode(r.x_m[...])
    r.send_ms[...] = packed_rows(nseq, group, {0: peak})
    send_all("m")
    send_all("ms")

    arrived("t")
    for i, row in enumerate(channel_rows(r.got_t[...].reshape(nseq, 128), 9, group)):
        r.taps_row[i : i + 1, :] = row

    @pl.when(me > 0)
    def _():
        for copy in halo_copies:
            copy.wait_recv()

    def tap_row(s, i):
        return r.taps_row[3 * s + i : 3 * s + i + 1, :]

    for s, src in enumerate([r.q, r.k, r.v]):
        own = src[...].astype(F32)
        above = r.halo[s].astype(F32)
        r.conv_rows[s] = (
            tap_row(s, 0) * own
            + tap_row(s, 1) * later(own, above, 1)
            + tap_row(s, 2) * later(own, above, 2)
        )

    arrived("qc")
    both = r.got_qc[...].astype(F32)
    r.x_q[...] = both[:, :group]
    r.x_c[...] = both[:, group:]
    r.x_g[...] = r.x_c[...] * short(r.x_q[...], r.d_q, taps[0])
    forward(r.x_g[...], r.spec_g)
    r.x_pg[...] = inverse(r.spec_h, r.spec_g, True) + gain * r.x_g[...]
    r.send_p[...], peak = encode(r.x_pg[...])
    r.send_ps[...] = packed_rows(nseq, group, {0: peak})
    send_all("p")
    send_all("ps")
    r.send_f[...], peak = encode(scale * inverse(r.spec_p, r.spec_g, True))
    r.send_fs[...] = packed_rows(nseq, group, {0: peak})
    send_all("f")
    send_all("fs")

    grads = [
        (r.x_c[...] * r.x_m[...], r.x_q, r.d_q),
        (r.x_pg[...] * r.value_conv[...], r.x_k, r.d_k),
        (r.x_pg[...] * r.key_conv[...], r.x_v, r.d_v),
    ]
    fields = {9: scale * total_of(r.x_g[...] * r.x_p[...])}
    for s, (grad, stream, moved) in enumerate(grads):
        fields[3 * s] = scale * total_of(grad * stream[...])
        fields[3 * s + 1] = scale * total_of(grad * moved[0])
        fields[3 * s + 2] = scale * total_of(grad * moved[1])
        fields[10 + 2 * s], fields[11 + 2 * s] = block_ends(grad, taps[s])
    r.send_s[...] = packed_rows(nseq, group, fields)
    send_all("s")

    def spread(grad, s):
        return (
            tap_row(s, 0) * grad
            + tap_row(s, 1) * pltpu.roll(grad, rows - 1, 0)
            + tap_row(s, 2) * pltpu.roll(grad, rows - 2, 0)
        ).astype(BF16)

    def in_rows(name):
        peaks = unpacked(getattr(r, "got_" + name + "s")[...], group, 0)
        return decode(getattr(r, "got_" + name)[...], peaks).reshape(rows, width).T

    arrived("m")
    arrived("ms")
    mixed = in_rows("m")
    r.go[...] = (r.conv_rows[0] * mixed).astype(BF16)
    r.qg[...] = spread(r.c[...].astype(F32) * mixed, 0)
    arrived("p")
    arrived("ps")
    product_grad = in_rows("p")
    r.kg[...] = spread(product_grad * r.conv_rows[2], 1)
    r.vg[...] = spread(product_grad * r.conv_rows[1], 2)
    arrived("f")
    arrived("fs")
    r.fg[...] = in_rows("f")
    arrived("s")
    r.sums[...] = r.got_s[...]

    for name in MESSAGES:
        sent(name)

    @pl.when(me < nseq - 1)
    def _():
        for copy in halo_copies:
            copy.wait_send()


def deliver(go, qg, kg, vg, fg, sums, go_out, qg_out, kg_out, vg_out, fg_out, taps_out, gain_out, ends, sem):
    nseq, group = sums.shape[0], gain_out.shape[1] // sums.shape[0]
    top = pl.ds(0, qg.shape[0] - HALO)
    low = pl.ds(qg.shape[0] - HALO, HALO)
    copies = [
        pltpu.make_async_copy(go, go_out, sem.at[0]),
        pltpu.make_async_copy(fg, fg_out, sem.at[1]),
    ]
    streams = [(qg, qg_out), (kg, kg_out), (vg, vg_out)]
    for i, (src, dst) in enumerate(streams):
        copies.append(pltpu.make_async_copy(src.at[top], dst.at[top], sem.at[2 + i]))
    for copy in copies:
        copy.start()
    rows = channel_rows(sums[...].reshape(nseq, 128), 16, group)
    place = lax.broadcasted_iota(jnp.int32, (HALO, qg.shape[1]), 0)
    for i, (src, dst) in enumerate(streams):
        last = src[low, :].astype(F32)
        last = jnp.where(place == HALO - 2, rows[10 + 2 * i], last)
        last = jnp.where(place == HALO - 1, rows[11 + 2 * i], last)
        ends[i] = last.astype(BF16)
        copy = pltpu.make_async_copy(ends.at[i], dst.at[low], sem.at[5 + i])
        copy.start()
        copies.append(copy)
    for i in range(9):
        taps_out[i // 3, i % 3 : i % 3 + 1, :] = rows[i]
    gain_out[...] = rows[9]
    for copy in copies:
        copy.wait()


def per_device(query_rows, key_rows, value_rows, long_filter, short_taps, skip_gain, cotangent):
    rows, channels = query_rows.shape
    nseq, nchan = lax.axis_size("seq"), lax.axis_size("chan")
    group = channels // nseq
    scale = 1.0 / math.sqrt(rows * nseq)
    tables = [jnp.asarray(t) for t in transform_tables(nseq, rows, group)]
    vmem = pl.BlockSpec(memory_space=pltpu.VMEM)
    hbm = pl.BlockSpec(memory_space=pltpu.HBM)
    inputs = {
        "q_hbm": query_rows,
        "k_hbm": key_rows,
        "v_hbm": value_rows,
        "c_hbm": cotangent,
        "h_hbm": long_filter,
        "taps_hbm": short_taps,
        "gain_hbm": skip_gain[None],
        "left_hbm": tables[0],
        "back_hbm": tables[1],
        "right_hbm": tables[2],
        "twist_hbm": tables[3],
    }
    block = jax.ShapeDtypeStruct((rows, channels), BF16)
    results = {
        "go": block,
        "qg": block,
        "kg": block,
        "vg": block,
        "fg": jax.ShapeDtypeStruct((rows, channels), F32),
        "sums": jax.ShapeDtypeStruct((nseq, 1, 128), F32),
    }
    local = pltpu.VMEM((rows, channels), BF16)
    taps, gain = pltpu.VMEM((3, 3, group), F32), pltpu.VMEM((1, group), F32)
    scratch = dict(
        q=local,
        k=local,
        v=local,
        c=local,
        h=pltpu.VMEM((rows, channels), F32),
        taps_own=taps,
        gain_own=gain,
        taps=taps,
        gain=gain,
        halo=pltpu.VMEM((3, HALO, channels), BF16),
        taps_row=pltpu.VMEM((16, channels), F32),
        conv_rows=pltpu.VMEM((3, rows, channels), F32),
    )
    for name, table in zip(("left", "back", "right", "twist"), tables):
        scratch[name] = pltpu.VMEM(table.shape, table.dtype)
    for name in MESSAGES:
        if name in ("kv", "qc"):
            kind = pltpu.VMEM((nseq, 2 * group, rows), BF16)
        elif name in ("h", "m", "p", "f"):
            kind = pltpu.VMEM((nseq, 2 * group, rows // 2), BF16)
        else:
            kind = pltpu.VMEM((nseq, 1, 128), F32)
        scratch["send_" + name] = scratch["got_" + name] = kind
    for name in ("x_q", "x_k", "x_v", "x_c", "x_p", "x_g", "x_m", "x_pg", "key_conv", "value_conv"):
        scratch[name] = pltpu.VMEM((nseq, group, rows), F32)
    for name in ("d_q", "d_k", "d_v"):
        scratch[name] = pltpu.VMEM((2, nseq, group, rows), F32)
    for name in ("spec_h", "spec_p", "spec_g"):
        scratch[name] = pltpu.VMEM((2, nseq * group, rows), F32)
    scratch["fetch_sem"] = pltpu.SemaphoreType.DMA((11,))
    scratch["send_sem"] = pltpu.SemaphoreType.DMA((len(MESSAGES),))
    scratch["recv_sem"] = pltpu.SemaphoreType.DMA((len(MESSAGES),))
    scratch["side_sem"] = pltpu.SemaphoreType.DMA((4,))
    scratch["halo_sem"] = pltpu.SemaphoreType.DMA((6,))
    names = tuple(inputs) + tuple(results) + tuple(scratch)
    outs = pl.pallas_call(
        functools.partial(kernel, names, nseq, nchan, group, scale),
        out_shape=tuple(results.values()),
        in_specs=[hbm] * len(inputs),
        out_specs=[vmem] * len(results),
        scratch_shapes=list(scratch.values()),
        compiler_params=pltpu.CompilerParams(
            collective_id=0, has_side_effects=True, vmem_limit_bytes=44 << 20
        ),
        name="hyena",
    )(*[pltpu.with_memory_space_constraint(x, pltpu.HBM) for x in inputs.values()])
    moved = pl.pallas_call(
        deliver,
        out_shape=tuple(jax.ShapeDtypeStruct(o.shape, o.dtype) for o in outs[:5])
        + (
            jax.ShapeDtypeStruct((3, 3, channels), F32),
            jax.ShapeDtypeStruct((1, channels), F32),
        ),
        in_specs=[vmem] * 6,
        out_specs=[hbm] * 5 + [vmem] * 2,
        scratch_shapes=[pltpu.VMEM((3, HALO, channels), BF16), pltpu.SemaphoreType.DMA((8,))],
        compiler_params=pltpu.CompilerParams(vmem_limit_bytes=16 << 20),
        name="deliver",
    )(*outs)
    return tuple(moved[:6]) + (moved[6].reshape(channels),)


def solution(mesh):
    in_specs = (
        P("seq", "chan"),
        P("seq", "chan"),
        P("seq", "chan"),
        P("seq", "chan"),
        P(None, None, ("seq", "chan")),
        P(("seq", "chan")),
        P("seq", "chan"),
    )
    out_specs = (
        P("seq", "chan"),
        P("seq", "chan"),
        P("seq", "chan"),
        P("seq", "chan"),
        P("seq", "chan"),
        P(None, None, "chan"),
        P("chan"),
    )
    return jax.shard_map(
        per_device, mesh=mesh, in_specs=in_specs, out_specs=out_specs, check_vma=False
    )
```

time: 69.2 us -> 48.2 us (0.70)
  local copies, waits for them, and re-layouts: 14.5 us -> 0 us
  Pallas kernels: 53.5 us -> 47.5 us
    unnamed x25 -> x0, local copies, waits for them, and re-layouts: 12.1 us -> none
    pallas_call x1 -> x2, Pallas kernels: 53.5 us -> 47.5 us  [the longest x1 45.6 us: per_device(): pl.pallas_call(functools.partial(kernel, names, nseq, nchan, group, scale...]
    reshape x4 -> x0, local copies, waits for them, and re-layouts: 1.56 us -> none  [the longest x1 0.74 us: per_device(): skip_gain.reshape(1, group)]
where the time goes in v4:
time: 48.2 us; the launch traced here: 48.1 us
  Pallas kernels  47.5 us (99%)
  between operations  0.64 us (1%)
    pallas_call x1, Pallas kernels, per_device(): pl.pallas_call(functools.partial(kernel, names, nseq, nchan, group, scale...  45.6 us
    pallas_call x1, Pallas kernels, per_device(): pl.pallas_call(deliver, out_shape=tuple((jax.ShapeDtypeStruct(o.shape, o....  1.91 us

profile of v4, /device:TPU:16, one launch (start us, length us, event | category | flops | bytes accessed | tf_op | source)
XLA Modules:
  0.0 48.1 jit_solution(450509104285395396)
XLA Ops:
  0.6 45.6 %hyena.1 = (bf16[256,256]{1,0:T(8,128)(2,1)S(1)}, bf16[256,256]{1,0:T(8,128)(2,1)S(1)}, bf16[256,256]{1,0:T(8,128)(2,1)S(1)}, bf16[256,256]{1,0:T(8,128)(2,1)S(1...) custom-call(bf16[256,256]{1,0:T(8,128)(2,1)} %refs_0_.1, bf16[256,256]{1,0:T(8,128)(2,1)} %refs_1_.1, ...), custom_call_target="tpu_custom_call" | custom-call | tf_op jit(solution)/shard_map/hyena/pallas_call | solution.py:550
  46.2 1.9 %deliver.1 = (bf16[256,256]{1,0:T(8,128)(2,1)}, bf16[256,256]{1,0:T(8,128)(2,1)}, bf16[256,256]{1,0:T(8,128)(2,1)}, bf16[256,256]{1,0:T(8,128)(2,1)}, f32[256,25...) custom-call(bf16[256,256]{1,0:T(8,128)(2,1)S(1)} %get-tuple-element.20.go, ...), custom_call_target="tpu_custom_call" | custom-call | tf_op jit(solution)/shard_map/deliver/pallas_call | solution.py:561

commit v5 on v4

--- a/solution.py
+++ b/solution.py
@@ -35,7 +35,10 @@
     turn = 2.0 * np.pi / total * np.outer(shifted, np.arange(width))
     twist = np.stack([np.cos(turn), np.sin(turn)]).astype(np.float32)
     twist = np.repeat(twist, group, axis=1)
-    return halves(left), halves(back), right, twist
+    left, back = halves(left), halves(back)
+    left = np.concatenate([left[0], left[0], left[1]], axis=1)
+    back = np.concatenate([back[0], back[0], back[1]], axis=1)
+    return left, back, right, twist
 
 
 def split(value):
@@ -45,10 +48,6 @@
 
 def dot(left, right):
     return jnp.dot(left, right, preferred_element_type=F32)
-
-
-def dot3(left, right):
-    return dot(left[0], right[0]) + dot(left[0], right[1]) + dot(left[1], right[0])
 
 
 def delayed(value, steps):
@@ -128,19 +127,32 @@
     )
     channel = lax.broadcasted_iota(jnp.int32, (128, width), 1)
     pick = lax.rem(channel, group) == lax.broadcasted_iota(jnp.int32, (128, width), 0)
-    wide = jnp.dot(
-        turned,
-        pick.astype(F32),
-        preferred_element_type=F32,
-        precision=lax.Precision.HIGHEST,
-    ).reshape(count, owners, width)
+    pick = pick.astype(F32).astype(BF16)
+    high, low = split(turned)
+    wide = (dot(high, pick) + dot(low, pick)).reshape(count, owners, width)
     owner = lax.div(lax.broadcasted_iota(jnp.int32, (owners, width), 1), group)
     keep = owner == lax.broadcasted_iota(jnp.int32, (owners, width), 0)
     return [jnp.sum(jnp.where(keep, wide[f], 0.0), axis=0, keepdims=True) for f in range(count)]
 
 
 HALO = 16
-MESSAGES = ("kv", "h", "hs", "qc", "t", "m", "ms", "p", "ps", "f", "fs", "s")
+DEPTH = 8
+
+
+def farthest(step, length):
+    away_by = lax.div(step + 1, 2)
+    return jnp.where(lax.rem(step, 2) == 1, length // 2 - away_by, length // 2 + away_by)
+
+
+def away(me, step, count):
+    planes = count // DEPTH
+    across = farthest(lax.div(step - 1, DEPTH), planes)
+    along = farthest(lax.rem(step - 1, DEPTH), DEPTH)
+    plane = lax.rem(lax.div(me, DEPTH) + across, planes)
+    return DEPTH * plane + lax.rem(lax.rem(me, DEPTH) + along, DEPTH)
+
+
+MESSAGES = ("kv", "h", "hs", "qc", "m", "ms", "p", "f", "pfs", "s")
 
 
 def kernel(names, nseq, nchan, group, scale, *refs):
@@ -206,7 +218,7 @@
         index = number[name]
 
         def body(step, carry):
-            peer = lax.rem(me + step, nseq)
+            peer = away(me, step, nseq)
             pltpu.make_async_remote_copy(
                 src_ref=source.at[peer],
                 dst_ref=target.at[me],
@@ -299,44 +311,54 @@
 
     taps = [[column(r.taps[s, i : i + 1, :]) for i in range(3)] for s in range(3)]
     gain = column(r.gain[...])
-    r.send_t[...] = jnp.broadcast_to(
-        packed_rows(1, group, {3 * s + i: taps[s][i] for s in range(3) for i in range(3)}),
-        r.send_t.shape,
-    )
-    send_all("t")
-
     for name in ("left", "twist", "right", "back"):
         fetched[name].wait()
 
+    high_cos, low_cos = r.right[0, 0], r.right[0, 1]
+    high_sin, low_sin = r.right[1, 0], r.right[1, 1]
+    for i, (cos_part, sin_part) in enumerate(
+        [(high_cos, high_sin), (high_cos, high_sin), (low_cos, low_sin)]
+    ):
+        top, bottom = pl.ds(i * width, width), pl.ds((3 + i) * width, width)
+        r.turn[top, :width] = cos_part
+        r.turn[bottom, :width] = sin_part
+        r.turn[top, width:] = -sin_part
+        r.turn[bottom, width:] = cos_part
+
+    def over_lanes(real, imag):
+        for i, value in enumerate([real, imag]):
+            high, low = split(value)
+            for k, part in enumerate([high, low, high]):
+                start = (3 * i + k) * width
+                r.lanes[:, start : start + width] = part
+        both = dot(r.lanes[...], r.turn[...])
+        return both[:, :width], both[:, width:]
+
     def forward(signal, spec):
-        parts = split(signal.reshape(rows, width))
-        wave = dot3((r.left[0], r.left[1]), parts)
+        high, low = split(signal.reshape(rows, width))
+        for i, part in enumerate([high, low, high]):
+            r.stack[i * rows : (i + 1) * rows, :] = part
+        wave = dot(r.left[...], r.stack[: 3 * rows, :])
         real, imag = wave[:rows], wave[rows:]
         cosine, sine = r.twist[0], r.twist[1]
-        turned_real = split(real * cosine + imag * sine)
-        turned_imag = split(imag * cosine - real * sine)
-        cos_parts = (r.right[0, 0], r.right[0, 1])
-        sin_parts = (r.right[1, 0], r.right[1, 1])
-        spec[0] = dot3(turned_real, cos_parts) + dot3(turned_imag, sin_parts)
-        spec[1] = dot3(turned_imag, cos_parts) - dot3(turned_real, sin_parts)
+        spec[0], spec[1] = over_lanes(
+            real * cosine + imag * sine, imag * cosine - real * sine
+        )
 
     def inverse(left_spec, right_spec, conjugate):
         a_re, a_im, b_re, b_im = left_spec[0], left_spec[1], right_spec[0], right_spec[1]
         if conjugate:
-            real, imag = a_re * b_re + a_im * b_im, a_re * b_im - a_im * b_re
+            real, imag = a_re * b_re + a_im * b_im, a_im * b_re - a_re * b_im
         else:
-            real, imag = a_re * b_re - a_im * b_im, a_re * b_im + a_im * b_re
-        real, imag = split(real), split(imag)
-        cos_parts = (r.right[0, 0], r.right[0, 1])
-        sin_parts = (r.right[1, 0], r.right[1, 1])
-        wave_real = dot3(real, cos_parts) - dot3(imag, sin_parts)
-        wave_imag = dot3(imag, cos_parts) + dot3(real, sin_parts)
+            real, imag = a_re * b_re - a_im * b_im, -(a_re * b_im + a_im * b_re)
+        wave_real, wave_imag = over_lanes(real, imag)
         cosine, sine = r.twist[0], r.twist[1]
-        turned_real = split(wave_real * cosine - wave_imag * sine)
-        turned_imag = split(wave_imag * cosine + wave_real * sine)
-        signal = dot3((r.back[0, :, :rows], r.back[1, :, :rows]), turned_real)
-        signal = signal + dot3((r.back[0, :, rows:], r.back[1, :, rows:]), turned_imag)
-        return signal.reshape(shape)
+        high_real, low_real = split(wave_real * cosine + wave_imag * sine)
+        high_imag, low_imag = split(wave_real * sine - wave_imag * cosine)
+        parts = [high_real, high_imag, low_real, low_imag, high_real, high_imag]
+        for i, part in enumerate(parts):
+            r.stack[i * rows : (i + 1) * rows, :] = part
+        return dot(r.back[...], r.stack[...]).reshape(shape)
 
     def short(value, keep, coeffs):
         one, two = delayed(value, 1), delayed(value, 2)
@@ -358,30 +380,10 @@
     forward(decode(r.got_h[...], unpacked(r.got_hs[...], group, 0)), r.spec_h)
     r.x_m[...] = inverse(r.spec_h, r.spec_p, False) + gain * r.x_p[...]
     r.send_m[...], peak = encode(r.x_m[...])
-    r.send_ms[...] = packed_rows(nseq, group, {0: peak})
+    fields = {3 * s + i: taps[s][i] for s in range(3) for i in range(3)}
+    r.send_ms[...] = packed_rows(nseq, group, {**fields, 9: peak})
     send_all("m")
     send_all("ms")
-
-    arrived("t")
-    for i, row in enumerate(channel_rows(r.got_t[...].reshape(nseq, 128), 9, group)):
-        r.taps_row[i : i + 1, :] = row
-
-    @pl.when(me > 0)
-    def _():
-        for copy in halo_copies:
-            copy.wait_recv()
-
-    def tap_row(s, i):
-        return r.taps_row[3 * s + i : 3 * s + i + 1, :]
-
-    for s, src in enumerate([r.q, r.k, r.v]):
-        own = src[...].astype(F32)
-        above = r.halo[s].astype(F32)
-        r.conv_rows[s] = (
-            tap_row(s, 0) * own
-            + tap_row(s, 1) * later(own, above, 1)
-            + tap_row(s, 2) * later(own, above, 2)
-        )
 
     arrived("qc")
     both = r.got_qc[...].astype(F32)
@@ -391,13 +393,11 @@
     forward(r.x_g[...], r.spec_g)
     r.x_pg[...] = inverse(r.spec_h, r.spec_g, True) + gain * r.x_g[...]
     r.send_p[...], peak = encode(r.x_pg[...])
-    r.send_ps[...] = packed_rows(nseq, group, {0: peak})
     send_all("p")
-    send_all("ps")
-    r.send_f[...], peak = encode(scale * inverse(r.spec_p, r.spec_g, True))
-    r.send_fs[...] = packed_rows(nseq, group, {0: peak})
+    r.send_f[...], other = encode(scale * inverse(r.spec_p, r.spec_g, True))
     send_all("f")
-    send_all("fs")
+    r.send_pfs[...] = packed_rows(nseq, group, {0: peak, 1: other})
+    send_all("pfs")
 
     grads = [
         (r.x_c[...] * r.x_m[...], r.x_q, r.d_q),
@@ -420,23 +420,42 @@
             + tap_row(s, 2) * pltpu.roll(grad, rows - 2, 0)
         ).astype(BF16)
 
-    def in_rows(name):
-        peaks = unpacked(getattr(r, "got_" + name + "s")[...], group, 0)
+    def in_rows(name, side, field):
+        peaks = unpacked(getattr(r, "got_" + side)[...], group, field)
         return decode(getattr(r, "got_" + name)[...], peaks).reshape(rows, width).T
 
+    arrived("ms")
+    for i, row in enumerate(channel_rows(r.got_ms[...].reshape(nseq, 128), 9, group)):
+        r.taps_row[i : i + 1, :] = row
+
+    @pl.when(me > 0)
+    def _():
+        for copy in halo_copies:
+            copy.wait_recv()
+
+    def tap_row(s, i):
+        return r.taps_row[3 * s + i : 3 * s + i + 1, :]
+
+    for s, src in enumerate([r.q, r.k, r.v]):
+        own = src[...].astype(F32)
+        above = r.halo[s].astype(F32)
+        r.conv_rows[s] = (
+            tap_row(s, 0) * own
+            + tap_row(s, 1) * later(own, above, 1)
+            + tap_row(s, 2) * later(own, above, 2)
+        )
+
     arrived("m")
-    arrived("ms")
-    mixed = in_rows("m")
+    mixed = in_rows("m", "ms", 9)
     r.go[...] = (r.conv_rows[0] * mixed).astype(BF16)
     r.qg[...] = spread(r.c[...].astype(F32) * mixed, 0)
     arrived("p")
-    arrived("ps")
-    product_grad = in_rows("p")
+    arrived("pfs")
+    product_grad = in_rows("p", "pfs", 0)
     r.kg[...] = spread(product_grad * r.conv_rows[2], 1)
     r.vg[...] = spread(product_grad * r.conv_rows[1], 2)
     arrived("f")
-    arrived("fs")
-    r.fg[...] = in_rows("f")
+    r.fg[...] = in_rows("f", "pfs", 1)
     arrived("s")
     r.sums[...] = r.got_s[...]
 
@@ -541,6 +560,9 @@
         scratch[name] = pltpu.VMEM((2, nseq, group, rows), F32)
     for name in ("spec_h", "spec_p", "spec_g"):
         scratch[name] = pltpu.VMEM((2, nseq * group, rows), F32)
+    scratch["turn"] = pltpu.VMEM((6 * rows, 2 * rows), BF16)
+    scratch["lanes"] = pltpu.VMEM((nseq * group, 6 * rows), BF16)
+    scratch["stack"] = pltpu.VMEM((6 * nseq * group, rows), BF16)
     scratch["fetch_sem"] = pltpu.SemaphoreType.DMA((11,))
     scratch["send_sem"] = pltpu.SemaphoreType.DMA((len(MESSAGES),))
     scratch["recv_sem"] = pltpu.SemaphoreType.DMA((len(MESSAGES),))

time: 48.2 us -> 44.5 us (0.923)
  Pallas kernels: 47.5 us -> 43.5 us
    pallas_call x1, Pallas kernels: 45.6 us -> 41.8 us  [per_device(): pl.pallas_call(functools.partial(kernel, names, nseq, nchan, group, scale...]
where the time goes in v5:
time: 44.5 us; the launch traced here: 44.1 us
  Pallas kernels  43.5 us (98%)
  between operations  0.64 us (1%)
    pallas_call x1, Pallas kernels, per_device(): pl.pallas_call(functools.partial(kernel, names, nseq, nchan, group, scale...  41.8 us
    pallas_call x1, Pallas kernels, per_device(): pl.pallas_call(deliver, out_shape=tuple((jax.ShapeDtypeStruct(o.shape, o....  1.63 us

profile of v5, /device:TPU:16, one launch (start us, length us, event | category | flops | bytes accessed | tf_op | source)
XLA Modules:
  0.0 44.1 jit_solution(7075828078626498899)
XLA Ops:
  0.6 41.8 %hyena.1 = (bf16[256,256]{1,0:T(8,128)(2,1)S(1)}, bf16[256,256]{1,0:T(8,128)(2,1)S(1)}, bf16[256,256]{1,0:T(8,128)(2,1)S(1)}, bf16[256,256]{1,0:T(8,128)(2,1)S(1...) custom-call(bf16[256,256]{1,0:T(8,128)(2,1)} %refs_0_.1, bf16[256,256]{1,0:T(8,128)(2,1)} %refs_1_.1, ...), custom_call_target="tpu_custom_call" | custom-call | tf_op jit(solution)/shard_map/hyena/pallas_call | solution.py:572
  42.5 1.6 %deliver.1 = (bf16[256,256]{1,0:T(8,128)(2,1)}, bf16[256,256]{1,0:T(8,128)(2,1)}, bf16[256,256]{1,0:T(8,128)(2,1)}, bf16[256,256]{1,0:T(8,128)(2,1)}, f32[256,25...) custom-call(bf16[256,256]{1,0:T(8,128)(2,1)S(1)} %get-tuple-element.20.go, ...), custom_call_target="tpu_custom_call" | custom-call | tf_op jit(solution)/shard_map/deliver/pallas_call | solution.py:583

commit v6 on v5

--- a/solution.py
+++ b/solution.py
@@ -30,15 +30,21 @@
     eye = np.eye(group)
     left = np.concatenate([np.kron(np.cos(outer), eye), np.kron(-np.sin(outer), eye)], axis=0)
     back = left.T / total
-    inner = 2.0 * np.pi / width * (np.outer(np.arange(width), np.arange(width)) % width)
-    right = np.stack([halves(np.cos(inner)), halves(np.sin(inner))])
+    half = width // 2
+    inner = 2.0 * np.pi / half * (np.outer(np.arange(half), np.arange(half)) % half)
+    cosine, sine = halves(np.cos(inner)), halves(np.sin(inner))
+    right = np.concatenate(
+        [np.block([[cosine[i], -sine[i]], [sine[i], cosine[i]]]) for i in (0, 0, 1)]
+    )
+    step = 2.0 * np.pi / width * np.arange(half)
+    swing = np.stack([np.tile(f(step), (8, 1)) for f in (np.cos, np.sin)]).astype(np.float32)
     turn = 2.0 * np.pi / total * np.outer(shifted, np.arange(width))
     twist = np.stack([np.cos(turn), np.sin(turn)]).astype(np.float32)
     twist = np.repeat(twist, group, axis=1)
     left, back = halves(left), halves(back)
     left = np.concatenate([left[0], left[0], left[1]], axis=1)
     back = np.concatenate([back[0], back[0], back[1]], axis=1)
-    return left, back, right, twist
+    return left, back, right, twist, swing
 
 
 def split(value):
@@ -152,7 +158,7 @@
     return DEPTH * plane + lax.rem(lax.rem(me, DEPTH) + along, DEPTH)
 
 
-MESSAGES = ("kv", "h", "hs", "qc", "m", "ms", "p", "f", "pfs", "s")
+MESSAGES = ("kv", "h", "hs", "qc", "m", "ms", "p", "s", "f", "fs")
 
 
 def kernel(names, nseq, nchan, group, scale, *refs):
@@ -165,7 +171,7 @@
     fetched = {}
     pairs = [("k", "k"), ("v", "v"), ("h", "h"), ("q", "q"), ("c", "c"), ("taps", "taps_own")]
     pairs += [("gain", "gain_own"), ("left", "left"), ("twist", "twist")]
-    pairs += [("right", "right"), ("back", "back")]
+    pairs += [("right", "right"), ("back", "back"), ("swing", "swing")]
     for i, (src, dst) in enumerate(pairs):
         fetched[src] = pltpu.make_async_copy(
             getattr(r, src + "_hbm"), getattr(r, dst), r.fetch_sem.at[i]
@@ -311,28 +317,19 @@
 
     taps = [[column(r.taps[s, i : i + 1, :]) for i in range(3)] for s in range(3)]
     gain = column(r.gain[...])
-    for name in ("left", "twist", "right", "back"):
+    for name in ("left", "twist", "right", "back", "swing"):
         fetched[name].wait()
 
-    high_cos, low_cos = r.right[0, 0], r.right[0, 1]
-    high_sin, low_sin = r.right[1, 0], r.right[1, 1]
-    for i, (cos_part, sin_part) in enumerate(
-        [(high_cos, high_sin), (high_cos, high_sin), (low_cos, low_sin)]
-    ):
-        top, bottom = pl.ds(i * width, width), pl.ds((3 + i) * width, width)
-        r.turn[top, :width] = cos_part
-        r.turn[bottom, :width] = sin_part
-        r.turn[top, width:] = -sin_part
-        r.turn[bottom, width:] = cos_part
+    half = width // 2
+    swing = [r.swing[i, :1, :] for i in range(2)]
 
     def over_lanes(real, imag):
-        for i, value in enumerate([real, imag]):
-            high, low = split(value)
-            for k, part in enumerate([high, low, high]):
-                start = (3 * i + k) * width
-                r.lanes[:, start : start + width] = part
-        both = dot(r.lanes[...], r.turn[...])
-        return both[:, :width], both[:, width:]
+        high_real, low_real = split(real)
+        high_imag, low_imag = split(imag)
+        parts = [high_real, high_imag, low_real, low_imag, high_real, high_imag]
+        for i, part in enumerate(parts):
+            r.lanes[:, i * half : (i + 1) * half] = part
+        return dot(r.lanes[...], r.right[...])
 
     def forward(signal, spec):
         high, low = split(signal.reshape(rows, width))
@@ -341,17 +338,41 @@
         wave = dot(r.left[...], r.stack[: 3 * rows, :])
         real, imag = wave[:rows], wave[rows:]
         cosine, sine = r.twist[0], r.twist[1]
-        spec[0], spec[1] = over_lanes(
-            real * cosine + imag * sine, imag * cosine - real * sine
+        real, imag = real * cosine + imag * sine, imag * cosine - real * sine
+        gap_real, gap_imag = real[:, :half] - real[:, half:], imag[:, :half] - imag[:, half:]
+        spec[...] = over_lanes(
+            jnp.concatenate(
+                [
+                    real[:, :half] + real[:, half:],
+                    gap_real * swing[0] + gap_imag * swing[1],
+                ],
+                axis=0,
+            ),
+            jnp.concatenate(
+                [
+                    imag[:, :half] + imag[:, half:],
+                    gap_imag * swing[0] - gap_real * swing[1],
+                ],
+                axis=0,
+            ),
         )
 
     def inverse(left_spec, right_spec, conjugate):
-        a_re, a_im, b_re, b_im = left_spec[0], left_spec[1], right_spec[0], right_spec[1]
+        a_re, a_im = left_spec[:, :half], left_spec[:, half:]
+        b_re, b_im = right_spec[:, :half], right_spec[:, half:]
         if conjugate:
             real, imag = a_re * b_re + a_im * b_im, a_im * b_re - a_re * b_im
         else:
             real, imag = a_re * b_re - a_im * b_im, -(a_re * b_im + a_im * b_re)
-        wave_real, wave_imag = over_lanes(real, imag)
+        wave = over_lanes(real, imag)
+        even_real, even_imag = wave[:rows, :half], wave[:rows, half:]
+        odd_real, odd_imag = wave[rows:, :half], wave[rows:, half:]
+        odd_real, odd_imag = (
+            odd_real * swing[0] + odd_imag * swing[1],
+            odd_imag * swing[0] - odd_real * swing[1],
+        )
+        wave_real = jnp.concatenate([even_real + odd_real, even_real - odd_real], axis=1)
+        wave_imag = jnp.concatenate([even_imag + odd_imag, even_imag - odd_imag], axis=1)
         cosine, sine = r.twist[0], r.twist[1]
         high_real, low_real = split(wave_real * cosine + wave_imag * sine)
         high_imag, low_imag = split(wave_real * sine - wave_imag * cosine)
@@ -394,10 +415,6 @@
     r.x_pg[...] = inverse(r.spec_h, r.spec_g, True) + gain * r.x_g[...]
     r.send_p[...], peak = encode(r.x_pg[...])
     send_all("p")
-    r.send_f[...], other = encode(scale * inverse(r.spec_p, r.spec_g, True))
-    send_all("f")
-    r.send_pfs[...] = packed_rows(nseq, group, {0: peak, 1: other})
-    send_all("pfs")
 
     grads = [
         (r.x_c[...] * r.x_m[...], r.x_q, r.d_q),
@@ -410,8 +427,13 @@
         fields[3 * s + 1] = scale * total_of(grad * moved[0])
         fields[3 * s + 2] = scale * total_of(grad * moved[1])
         fields[10 + 2 * s], fields[11 + 2 * s] = block_ends(grad, taps[s])
-    r.send_s[...] = packed_rows(nseq, group, fields)
+    r.send_s[:, :, :128] = packed_rows(nseq, group, fields)
+    r.send_s[:, :, 128:] = packed_rows(nseq, group, {0: peak})
     send_all("s")
+    r.send_f[...], peak = encode(scale * inverse(r.spec_p, r.spec_g, True))
+    send_all("f")
+    r.send_fs[...] = packed_rows(nseq, group, {0: peak})
+    send_all("fs")
 
     def spread(grad, s):
         return (
@@ -421,8 +443,9 @@
         ).astype(BF16)
 
     def in_rows(name, side, field):
-        peaks = unpacked(getattr(r, "got_" + side)[...], group, field)
-        return decode(getattr(r, "got_" + name)[...], peaks).reshape(rows, width).T
+        return decode(getattr(r, "got_" + name)[...], unpacked(side, group, field)).reshape(
+            rows, width
+        ).T
 
     arrived("ms")
     for i, row in enumerate(channel_rows(r.got_ms[...].reshape(nseq, 128), 9, group)):
@@ -446,18 +469,27 @@
         )
 
     arrived("m")
-    mixed = in_rows("m", "ms", 9)
+    mixed = in_rows("m", r.got_ms[...], 9)
     r.go[...] = (r.conv_rows[0] * mixed).astype(BF16)
     r.qg[...] = spread(r.c[...].astype(F32) * mixed, 0)
     arrived("p")
-    arrived("pfs")
-    product_grad = in_rows("p", "pfs", 0)
+    arrived("s")
+    product_grad = in_rows("p", r.got_s[:, :, 128:], 0)
     r.kg[...] = spread(product_grad * r.conv_rows[2], 1)
     r.vg[...] = spread(product_grad * r.conv_rows[1], 2)
+    finals = channel_rows(r.got_s[:, :, :128].reshape(nseq, 128), 16, group)
+    place = lax.broadcasted_iota(jnp.int32, (HALO, width), 0)
+    for i, grad in enumerate([r.qg, r.kg, r.vg]):
+        last = grad[rows - HALO :, :].astype(F32)
+        last = jnp.where(place == HALO - 2, finals[10 + 2 * i], last)
+        last = jnp.where(place == HALO - 1, finals[11 + 2 * i], last)
+        grad[rows - HALO :, :] = last.astype(BF16)
+    for i in range(9):
+        r.taps_grad[i // 3, i % 3 : i % 3 + 1, :] = finals[i]
+    r.gain_grad[...] = finals[9]
     arrived("f")
-    r.fg[...] = in_rows("f", "pfs", 1)
-    arrived("s")
-    r.sums[...] = r.got_s[...]
+    arrived("fs")
+    r.fg[...] = in_rows("f", r.got_fs[...], 0)
 
     for name in MESSAGES:
         sent(name)
@@ -468,32 +500,13 @@
             copy.wait_send()
 
 
-def deliver(go, qg, kg, vg, fg, sums, go_out, qg_out, kg_out, vg_out, fg_out, taps_out, gain_out, ends, sem):
-    nseq, group = sums.shape[0], gain_out.shape[1] // sums.shape[0]
-    top = pl.ds(0, qg.shape[0] - HALO)
-    low = pl.ds(qg.shape[0] - HALO, HALO)
+def deliver(*refs):
+    count = len(refs) // 2
     copies = [
-        pltpu.make_async_copy(go, go_out, sem.at[0]),
-        pltpu.make_async_copy(fg, fg_out, sem.at[1]),
+        pltpu.make_async_copy(refs[i], refs[count + i], refs[-1].at[i]) for i in range(count)
     ]
-    streams = [(qg, qg_out), (kg, kg_out), (vg, vg_out)]
-    for i, (src, dst) in enumerate(streams):
-        copies.append(pltpu.make_async_copy(src.at[top], dst.at[top], sem.at[2 + i]))
     for copy in copies:
         copy.start()
-    rows = channel_rows(sums[...].reshape(nseq, 128), 16, group)
-    place = lax.broadcasted_iota(jnp.int32, (HALO, qg.shape[1]), 0)
-    for i, (src, dst) in enumerate(streams):
-        last = src[low, :].astype(F32)
-        last = jnp.where(place == HALO - 2, rows[10 + 2 * i], last)
-        last = jnp.where(place == HALO - 1, rows[11 + 2 * i], last)
-        ends[i] = last.astype(BF16)
-        copy = pltpu.make_async_copy(ends.at[i], dst.at[low], sem.at[5 + i])
-        copy.start()
-        copies.append(copy)
-    for i in range(9):
-        taps_out[i // 3, i % 3 : i % 3 + 1, :] = rows[i]
-    gain_out[...] = rows[9]
     for copy in copies:
         copy.wait()
 
@@ -518,6 +531,7 @@
         "back_hbm": tables[1],
         "right_hbm": tables[2],
         "twist_hbm": tables[3],
+        "swing_hbm": tables[4],
     }
     block = jax.ShapeDtypeStruct((rows, channels), BF16)
     results = {
@@ -526,7 +540,8 @@
         "kg": block,
         "vg": block,
         "fg": jax.ShapeDtypeStruct((rows, channels), F32),
-        "sums": jax.ShapeDtypeStruct((nseq, 1, 128), F32),
+        "taps_grad": jax.ShapeDtypeStruct((3, 3, channels), F32),
+        "gain_grad": jax.ShapeDtypeStruct((1, channels), F32),
     }
     local = pltpu.VMEM((rows, channels), BF16)
     taps, gain = pltpu.VMEM((3, 3, group), F32), pltpu.VMEM((1, group), F32)
@@ -544,7 +559,7 @@
         taps_row=pltpu.VMEM((16, channels), F32),
         conv_rows=pltpu.VMEM((3, rows, channels), F32),
     )
-    for name, table in zip(("left", "back", "right", "twist"), tables):
+    for name, table in zip(("left", "back", "right", "twist", "swing"), tables):
         scratch[name] = pltpu.VMEM(table.shape, table.dtype)
     for name in MESSAGES:
         if name in ("kv", "qc"):
@@ -552,18 +567,17 @@
         elif name in ("h", "m", "p", "f"):
             kind = pltpu.VMEM((nseq, 2 * group, rows // 2), BF16)
         else:
-            kind = pltpu.VMEM((nseq, 1, 128), F32)
+            kind = pltpu.VMEM((nseq, 1, 256 if name == "s" else 128), F32)
         scratch["send_" + name] = scratch["got_" + name] = kind
     for name in ("x_q", "x_k", "x_v", "x_c", "x_p", "x_g", "x_m", "x_pg", "key_conv", "value_conv"):
         scratch[name] = pltpu.VMEM((nseq, group, rows), F32)
     for name in ("d_q", "d_k", "d_v"):
         scratch[name] = pltpu.VMEM((2, nseq, group, rows), F32)
     for name in ("spec_h", "spec_p", "spec_g"):
-        scratch[name] = pltpu.VMEM((2, nseq * group, rows), F32)
-    scratch["turn"] = pltpu.VMEM((6 * rows, 2 * rows), BF16)
-    scratch["lanes"] = pltpu.VMEM((nseq * group, 6 * rows), BF16)
+        scratch[name] = pltpu.VMEM((2 * nseq * group, rows), F32)
+    scratch["lanes"] = pltpu.VMEM((2 * nseq * group, 3 * rows), BF16)
     scratch["stack"] = pltpu.VMEM((6 * nseq * group, rows), BF16)
-    scratch["fetch_sem"] = pltpu.SemaphoreType.DMA((11,))
+    scratch["fetch_sem"] = pltpu.SemaphoreType.DMA((12,))
     scratch["send_sem"] = pltpu.SemaphoreType.DMA((len(MESSAGES),))
     scratch["recv_sem"] = pltpu.SemaphoreType.DMA((len(MESSAGES),))
     scratch["side_sem"] = pltpu.SemaphoreType.DMA((4,))
@@ -582,14 +596,10 @@
     )(*[pltpu.with_memory_space_constraint(x, pltpu.HBM) for x in inputs.values()])
     moved = pl.pallas_call(
         deliver,
-        out_shape=tuple(jax.ShapeDtypeStruct(o.shape, o.dtype) for o in outs[:5])
-        + (
-            jax.ShapeDtypeStruct((3, 3, channels), F32),
-            jax.ShapeDtypeStruct((1, channels), F32),
-        ),
-        in_specs=[vmem] * 6,
-        out_specs=[hbm] * 5 + [vmem] * 2,
-        scratch_shapes=[pltpu.VMEM((3, HALO, channels), BF16), pltpu.SemaphoreType.DMA((8,))],
+        out_shape=tuple(results.values()),
+        in_specs=[vmem] * len(results),
+        out_specs=[hbm] * len(results),
+        scratch_shapes=[pltpu.SemaphoreType.DMA((len(results),))],
         compiler_params=pltpu.CompilerParams(vmem_limit_bytes=16 << 20),
         name="deliver",
     )(*outs)

time: 44.5 us -> 44.4 us (level)
    pallas_call x1, Pallas kernels: 41.8 us -> 42.7 us  [per_device(): pl.pallas_call(functools.partial(kernel, names, nseq, nchan, group, scale...]
    pallas_call x1, Pallas kernels: 1.63 us -> 0.94 us  [per_device(): pl.pallas_call(deliver, out_shape=tuple(results.values()), in_specs=[vmem...]
where the time goes in v6:
time: 44.4 us; the launch traced here: 44.3 us
  Pallas kernels  43.6 us (98%)
  between operations  0.64 us (1%)
    pallas_call x1, Pallas kernels, per_device(): pl.pallas_call(functools.partial(kernel, names, nseq, nchan, group, scale...  42.7 us
    pallas_call x1, Pallas kernels, per_device(): pl.pallas_call(deliver, out_shape=tuple(results.values()), in_specs=[vmem...  0.94 us

profile of v6, /device:TPU:16, one launch (start us, length us, event | category | flops | bytes accessed | tf_op | source)
XLA Modules:
  0.0 44.3 jit_solution(7813089351617327494)
XLA Ops:
  0.6 42.7 %hyena.1 = (bf16[256,256]{1,0:T(8,128)(2,1)S(1)}, bf16[256,256]{1,0:T(8,128)(2,1)S(1)}, bf16[256,256]{1,0:T(8,128)(2,1)S(1)}, bf16[256,256]{1,0:T(8,128)(2,1)S(1...) custom-call(bf16[256,256]{1,0:T(8,128)(2,1)} %refs_0_.1, bf16[256,256]{1,0:T(8,128)(2,1)} %refs_1_.1, ...), custom_call_target="tpu_custom_call" | custom-call | tf_op jit(solution)/shard_map/hyena/pallas_call | solution.py:586
  43.3 0.9 %deliver.1 = (bf16[256,256]{1,0:T(8,128)(2,1)}, bf16[256,256]{1,0:T(8,128)(2,1)}, bf16[256,256]{1,0:T(8,128)(2,1)}, bf16[256,256]{1,0:T(8,128)(2,1)}, f32[256,25...) custom-call(bf16[256,256]{1,0:T(8,128)(2,1)S(1)} %get-tuple-element.21.refs_0_, ...), custom_call_target="tpu_custom_call" | custom-call | tf_op jit(solution)/shard_map/deliver/pallas_call | solution.py:597

commit v7 on v6

--- a/solution.py
+++ b/solution.py
@@ -43,6 +43,7 @@
     twist = np.repeat(twist, group, axis=1)
     left, back = halves(left), halves(back)
     left = np.concatenate([left[0], left[0], left[1]], axis=1)
+    left = left.reshape(2, 2, -1, left.shape[1]).swapaxes(0, 1).reshape(left.shape)
     back = np.concatenate([back[0], back[0], back[1]], axis=1)
     return left, back, right, twist, swing
 
@@ -219,7 +220,7 @@
     def _():
         pl.semaphore_wait(barrier, nseq)
 
-    def send_all(name):
+    def send_all(name, unroll=1):
         source, target = getattr(r, "send_" + name), getattr(r, "got_" + name)
         index = number[name]
 
@@ -235,7 +236,7 @@
             ).start()
             return carry
 
-        lax.fori_loop(1, nseq, body, 0)
+        lax.fori_loop(1, nseq, body, 0, unroll=unroll)
         target[me] = source[me]
 
     def arrived(name):
@@ -323,62 +324,69 @@
     half = width // 2
     swing = [r.swing[i, :1, :] for i in range(2)]
 
-    def over_lanes(real, imag):
+    part_rows = rows // 2
+
+    def over_lanes(block, real, imag):
+        place = slice(block * rows, (block + 1) * rows)
         high_real, low_real = split(real)
         high_imag, low_imag = split(imag)
         parts = [high_real, high_imag, low_real, low_imag, high_real, high_imag]
         for i, part in enumerate(parts):
-            r.lanes[:, i * half : (i + 1) * half] = part
-        return dot(r.lanes[...], r.right[...])
+            r.lanes[place, i * half : (i + 1) * half] = part
+        return dot(r.lanes[place, :], r.right[...])
 
     def forward(signal, spec):
         high, low = split(signal.reshape(rows, width))
         for i, part in enumerate([high, low, high]):
             r.stack[i * rows : (i + 1) * rows, :] = part
-        wave = dot(r.left[...], r.stack[: 3 * rows, :])
-        real, imag = wave[:rows], wave[rows:]
-        cosine, sine = r.twist[0], r.twist[1]
-        real, imag = real * cosine + imag * sine, imag * cosine - real * sine
-        gap_real, gap_imag = real[:, :half] - real[:, half:], imag[:, :half] - imag[:, half:]
-        spec[...] = over_lanes(
-            jnp.concatenate(
-                [
-                    real[:, :half] + real[:, half:],
-                    gap_real * swing[0] + gap_imag * swing[1],
-                ],
-                axis=0,
-            ),
-            jnp.concatenate(
-                [
-                    imag[:, :half] + imag[:, half:],
-                    gap_imag * swing[0] - gap_real * swing[1],
-                ],
-                axis=0,
-            ),
-        )
+        waves = [
+            dot(r.left[block * rows : (block + 1) * rows, :], r.stack[: 3 * rows, :])
+            for block in range(2)
+        ]
+        for block, wave in enumerate(waves):
+            real, imag = wave[:part_rows], wave[part_rows:]
+            turn = slice(block * part_rows, (block + 1) * part_rows)
+            cosine, sine = r.twist[0, turn, :], r.twist[1, turn, :]
+            real, imag = real * cosine + imag * sine, imag * cosine - real * sine
+            gap_real = real[:, :half] - real[:, half:]
+            gap_imag = imag[:, :half] - imag[:, half:]
+            even_real, even_imag = real[:, :half] + real[:, half:], imag[:, :half] + imag[:, half:]
+            odd_real = gap_real * swing[0] + gap_imag * swing[1]
+            odd_imag = gap_imag * swing[0] - gap_real * swing[1]
+            spec[block * rows : (block + 1) * rows, :] = over_lanes(
+                block,
+                jnp.concatenate([even_real, odd_real], axis=0),
+                jnp.concatenate([even_imag, odd_imag], axis=0),
+            )
 
     def inverse(left_spec, right_spec, conjugate):
-        a_re, a_im = left_spec[:, :half], left_spec[:, half:]
-        b_re, b_im = right_spec[:, :half], right_spec[:, half:]
-        if conjugate:
-            real, imag = a_re * b_re + a_im * b_im, a_im * b_re - a_re * b_im
-        else:
-            real, imag = a_re * b_re - a_im * b_im, -(a_re * b_im + a_im * b_re)
-        wave = over_lanes(real, imag)
-        even_real, even_imag = wave[:rows, :half], wave[:rows, half:]
-        odd_real, odd_imag = wave[rows:, :half], wave[rows:, half:]
-        odd_real, odd_imag = (
-            odd_real * swing[0] + odd_imag * swing[1],
-            odd_imag * swing[0] - odd_real * swing[1],
-        )
-        wave_real = jnp.concatenate([even_real + odd_real, even_real - odd_real], axis=1)
-        wave_imag = jnp.concatenate([even_imag + odd_imag, even_imag - odd_imag], axis=1)
-        cosine, sine = r.twist[0], r.twist[1]
-        high_real, low_real = split(wave_real * cosine + wave_imag * sine)
-        high_imag, low_imag = split(wave_real * sine - wave_imag * cosine)
-        parts = [high_real, high_imag, low_real, low_imag, high_real, high_imag]
-        for i, part in enumerate(parts):
-            r.stack[i * rows : (i + 1) * rows, :] = part
+        waves = []
+        for block in range(2):
+            place = slice(block * rows, (block + 1) * rows)
+            a_re, a_im = left_spec[place, :half], left_spec[place, half:]
+            b_re, b_im = right_spec[place, :half], right_spec[place, half:]
+            if conjugate:
+                real, imag = a_re * b_re + a_im * b_im, a_im * b_re - a_re * b_im
+            else:
+                real, imag = a_re * b_re - a_im * b_im, -(a_re * b_im + a_im * b_re)
+            waves.append(over_lanes(block, real, imag))
+        for block, wave in enumerate(waves):
+            even_real, even_imag = wave[:part_rows, :half], wave[:part_rows, half:]
+            odd_real, odd_imag = wave[part_rows:, :half], wave[part_rows:, half:]
+            odd_real, odd_imag = (
+                odd_real * swing[0] + odd_imag * swing[1],
+                odd_imag * swing[0] - odd_real * swing[1],
+            )
+            wave_real = jnp.concatenate([even_real + odd_real, even_real - odd_real], axis=1)
+            wave_imag = jnp.concatenate([even_imag + odd_imag, even_imag - odd_imag], axis=1)
+            turn = slice(block * part_rows, (block + 1) * part_rows)
+            cosine, sine = r.twist[0, turn, :], r.twist[1, turn, :]
+            high_real, low_real = split(wave_real * cosine + wave_imag * sine)
+            high_imag, low_imag = split(wave_real * sine - wave_imag * cosine)
+            parts = [high_real, high_imag, low_real, low_imag, high_real, high_imag]
+            for i, part in enumerate(parts):
+                start = i * rows + block * part_rows
+                r.stack[start : start + part_rows, :] = part
         return dot(r.back[...], r.stack[...]).reshape(shape)
 
     def short(value, keep, coeffs):
@@ -414,7 +422,7 @@
     forward(r.x_g[...], r.spec_g)
     r.x_pg[...] = inverse(r.spec_h, r.spec_g, True) + gain * r.x_g[...]
     r.send_p[...], peak = encode(r.x_pg[...])
-    send_all("p")
+    send_all("p", nseq - 1)
 
     grads = [
         (r.x_c[...] * r.x_m[...], r.x_q, r.d_q),
@@ -429,7 +437,7 @@
         fields[10 + 2 * s], fields[11 + 2 * s] = block_ends(grad, taps[s])
     r.send_s[:, :, :128] = packed_rows(nseq, group, fields)
     r.send_s[:, :, 128:] = packed_rows(nseq, group, {0: peak})
-    send_all("s")
+    send_all("s", nseq - 1)
     r.send_f[...], peak = encode(scale * inverse(r.spec_p, r.spec_g, True))
     send_all("f")
     r.send_fs[...] = packed_rows(nseq, group, {0: peak})

time: 44.4 us -> 43.1 us (0.971)
  Pallas kernels: 43.6 us -> 42.3 us
    pallas_call x1, Pallas kernels: 42.7 us -> 41.4 us  [per_device(): pl.pallas_call(functools.partial(kernel, names, nseq, nchan, group, scale...]
where the time goes in v7:
time: 43.1 us; the launch traced here: 43 us
  Pallas kernels  42.3 us (98%)
  between operations  0.64 us (1%)
    pallas_call x1, Pallas kernels, per_device(): pl.pallas_call(functools.partial(kernel, names, nseq, nchan, group, scale...  41.4 us
    pallas_call x1, Pallas kernels, per_device(): pl.pallas_call(deliver, out_shape=tuple(results.values()), in_specs=[vmem...  0.94 us

profile of v7, /device:TPU:16, one launch (start us, length us, event | category | flops | bytes accessed | tf_op | source)
XLA Modules:
  0.0 43.0 jit_solution(17161098949040392025)
XLA Ops:
  0.6 41.4 %hyena.1 = (bf16[256,256]{1,0:T(8,128)(2,1)S(1)}, bf16[256,256]{1,0:T(8,128)(2,1)S(1)}, bf16[256,256]{1,0:T(8,128)(2,1)S(1)}, bf16[256,256]{1,0:T(8,128)(2,1)S(1...) custom-call(bf16[256,256]{1,0:T(8,128)(2,1)} %refs_0_.1, bf16[256,256]{1,0:T(8,128)(2,1)} %refs_1_.1, ...), custom_call_target="tpu_custom_call" | custom-call | tf_op jit(solution)/shard_map/hyena/pallas_call | solution.py:594
  42.0 0.9 %deliver.1 = (bf16[256,256]{1,0:T(8,128)(2,1)}, bf16[256,256]{1,0:T(8,128)(2,1)}, bf16[256,256]{1,0:T(8,128)(2,1)}, bf16[256,256]{1,0:T(8,128)(2,1)}, f32[256,25...) custom-call(bf16[256,256]{1,0:T(8,128)(2,1)S(1)} %get-tuple-element.21.refs_0_, ...), custom_call_target="tpu_custom_call" | custom-call | tf_op jit(solution)/shard_map/deliver/pallas_call | solution.py:605

commit v8 on v7

--- a/solution.py
+++ b/solution.py
@@ -159,7 +159,7 @@
     return DEPTH * plane + lax.rem(lax.rem(me, DEPTH) + along, DEPTH)
 
 
-MESSAGES = ("kv", "h", "hs", "qc", "m", "ms", "p", "s", "f", "fs")
+MESSAGES = ("kv", "h", "hs", "qc", "m", "p", "s", "f", "fs")
 
 
 def kernel(names, nseq, nchan, group, scale, *refs):
@@ -409,10 +409,9 @@
     forward(decode(r.got_h[...], unpacked(r.got_hs[...], group, 0)), r.spec_h)
     r.x_m[...] = inverse(r.spec_h, r.spec_p, False) + gain * r.x_p[...]
     r.send_m[...], peak = encode(r.x_m[...])
-    fields = {3 * s + i: taps[s][i] for s in range(3) for i in range(3)}
-    r.send_ms[...] = packed_rows(nseq, group, {**fields, 9: peak})
     send_all("m")
-    send_all("ms")
+    fields = {2 + 3 * s + i: taps[s][i] for s in range(3) for i in range(3)}
+    r.send_s[:, :, 128:] = packed_rows(nseq, group, {**fields, 1: peak})
 
     arrived("qc")
     both = r.got_qc[...].astype(F32)
@@ -436,7 +435,7 @@
         fields[3 * s + 2] = scale * total_of(grad * moved[1])
         fields[10 + 2 * s], fields[11 + 2 * s] = block_ends(grad, taps[s])
     r.send_s[:, :, :128] = packed_rows(nseq, group, fields)
-    r.send_s[:, :, 128:] = packed_rows(nseq, group, {0: peak})
+    r.send_s[:, :, 128:] = r.send_s[:, :, 128:] + packed_rows(nseq, group, {0: peak})
     send_all("s", nseq - 1)
     r.send_f[...], peak = encode(scale * inverse(r.spec_p, r.spec_g, True))
     send_all("f")
@@ -455,8 +454,9 @@
             rows, width
         ).T
 
-    arrived("ms")
-    for i, row in enumerate(channel_rows(r.got_ms[...].reshape(nseq, 128), 9, group)):
+    arrived("s")
+    side = r.got_s[:, :, 128:]
+    for i, row in enumerate(channel_rows(side.reshape(nseq, 128), 11, group)[2:]):
         r.taps_row[i : i + 1, :] = row
 
     @pl.when(me > 0)
@@ -477,11 +477,10 @@
         )
 
     arrived("m")
-    mixed = in_rows("m", r.got_ms[...], 9)
+    mixed = in_rows("m", side, 1)
     r.go[...] = (r.conv_rows[0] * mixed).astype(BF16)
     r.qg[...] = spread(r.c[...].astype(F32) * mixed, 0)
     arrived("p")
-    arrived("s")
     product_grad = in_rows("p", r.got_s[:, :, 128:], 0)
     r.kg[...] = spread(product_grad * r.conv_rows[2], 1)
     r.vg[...] = spread(product_grad * r.conv_rows[1], 2)

time: 43.1 us -> 43 us (level)
  no operation moved by 1% of the time
where the time goes in v8:
time: 43 us
  Pallas kernels  42.3 us (98%)
  between operations  0.64 us (1%)
    pallas_call x1, Pallas kernels, per_device(): pl.pallas_call(functools.partial(kernel, names, nseq, nchan, group, scale...  41.4 us
    pallas_call x1, Pallas kernels, per_device(): pl.pallas_call(deliver, out_shape=tuple(results.values()), in_specs=[vmem...  0.94 us

profile of v8, /device:TPU:16, one launch (start us, length us, event | category | flops | bytes accessed | tf_op | source)
XLA Modules:
  0.0 43.0 jit_solution(8226846531670779853)
XLA Ops:
  0.6 41.4 %hyena.1 = (bf16[256,256]{1,0:T(8,128)(2,1)S(1)}, bf16[256,256]{1,0:T(8,128)(2,1)S(1)}, bf16[256,256]{1,0:T(8,128)(2,1)S(1)}, bf16[256,256]{1,0:T(8,128)(2,1)S(1...) custom-call(bf16[256,256]{1,0:T(8,128)(2,1)} %refs_0_.1, bf16[256,256]{1,0:T(8,128)(2,1)} %refs_1_.1, ...), custom_call_target="tpu_custom_call" | custom-call | tf_op jit(solution)/shard_map/hyena/pallas_call | solution.py:593
  42.0 0.9 %deliver.1 = (bf16[256,256]{1,0:T(8,128)(2,1)}, bf16[256,256]{1,0:T(8,128)(2,1)}, bf16[256,256]{1,0:T(8,128)(2,1)}, bf16[256,256]{1,0:T(8,128)(2,1)}, f32[256,25...) custom-call(bf16[256,256]{1,0:T(8,128)(2,1)S(1)} %get-tuple-element.21.refs_0_, ...), custom_call_target="tpu_custom_call" | custom-call | tf_op jit(solution)/shard_map/deliver/pallas_call | solution.py:604

commit v9 on v8

--- a/solution.py
+++ b/solution.py
@@ -449,14 +449,16 @@
             + tap_row(s, 2) * pltpu.roll(grad, rows - 2, 0)
         ).astype(BF16)
 
-    def in_rows(name, side, field):
-        return decode(getattr(r, "got_" + name)[...], unpacked(side, group, field)).reshape(
-            rows, width
-        ).T
+    def in_rows(name, peaks):
+        return decode(getattr(r, "got_" + name)[...], peaks).reshape(rows, width).T
+
+    unit = jnp.ones((nseq, group, 1), F32)
+    arrived("m")
+    r.mixed_rows[...] = in_rows("m", unit)
 
     arrived("s")
     side = r.got_s[:, :, 128:]
-    for i, row in enumerate(channel_rows(side.reshape(nseq, 128), 11, group)[2:]):
+    for i, row in enumerate(channel_rows(side.reshape(nseq, 128), 11, group)):
         r.taps_row[i : i + 1, :] = row
 
     @pl.when(me > 0)
@@ -465,7 +467,7 @@
             copy.wait_recv()
 
     def tap_row(s, i):
-        return r.taps_row[3 * s + i : 3 * s + i + 1, :]
+        return r.taps_row[2 + 3 * s + i : 3 + 3 * s + i, :]
 
     for s, src in enumerate([r.q, r.k, r.v]):
         own = src[...].astype(F32)
@@ -476,12 +478,11 @@
             + tap_row(s, 2) * later(own, above, 2)
         )
 
-    arrived("m")
-    mixed = in_rows("m", side, 1)
+    mixed = r.mixed_rows[...] * r.taps_row[1:2, :]
     r.go[...] = (r.conv_rows[0] * mixed).astype(BF16)
     r.qg[...] = spread(r.c[...].astype(F32) * mixed, 0)
     arrived("p")
-    product_grad = in_rows("p", r.got_s[:, :, 128:], 0)
+    product_grad = in_rows("p", unit) * r.taps_row[0:1, :]
     r.kg[...] = spread(product_grad * r.conv_rows[2], 1)
     r.vg[...] = spread(product_grad * r.conv_rows[1], 2)
     finals = channel_rows(r.got_s[:, :, :128].reshape(nseq, 128), 16, group)
@@ -496,7 +497,7 @@
     r.gain_grad[...] = finals[9]
     arrived("f")
     arrived("fs")
-    r.fg[...] = in_rows("f", r.got_fs[...], 0)
+    r.fg[...] = in_rows("f", unpacked(r.got_fs[...], group, 0))
 
     for name in MESSAGES:
         sent(name)
@@ -564,6 +565,7 @@
         gain=gain,
         halo=pltpu.VMEM((3, HALO, channels), BF16),
         taps_row=pltpu.VMEM((16, channels), F32),
+        mixed_rows=pltpu.VMEM((rows, channels), F32),
         conv_rows=pltpu.VMEM((3, rows, channels), F32),
     )
     for name, table in zip(("left", "back", "right", "twist", "swing"), tables):

time: 43 us -> 43 us (level)
  no operation moved by 1% of the time
where the time goes in v9:
time: 43 us
  Pallas kernels  42.3 us (98%)
  between operations  0.64 us (1%)
    pallas_call x1, Pallas kernels, per_device(): pl.pallas_call(functools.partial(kernel, names, nseq, nchan, group, scale...  41.4 us
    pallas_call x1, Pallas kernels, per_device(): pl.pallas_call(deliver, out_shape=tuple(results.values()), in_specs=[vmem...  0.94 us

profile of v9, /device:TPU:16, one launch (start us, length us, event | category | flops | bytes accessed | tf_op | source)
XLA Modules:
  0.0 43.0 jit_solution(14732561230887433978)
XLA Ops:
  0.6 41.4 %hyena.1 = (bf16[256,256]{1,0:T(8,128)(2,1)S(1)}, bf16[256,256]{1,0:T(8,128)(2,1)S(1)}, bf16[256,256]{1,0:T(8,128)(2,1)S(1)}, bf16[256,256]{1,0:T(8,128)(2,1)S(1...) custom-call(bf16[256,256]{1,0:T(8,128)(2,1)} %refs_0_.1, bf16[256,256]{1,0:T(8,128)(2,1)} %refs_1_.1, ...), custom_call_target="tpu_custom_call" | custom-call | tf_op jit(solution)/shard_map/hyena/pallas_call | solution.py:595
  42.0 0.9 %deliver.1 = (bf16[256,256]{1,0:T(8,128)(2,1)}, bf16[256,256]{1,0:T(8,128)(2,1)}, bf16[256,256]{1,0:T(8,128)(2,1)}, bf16[256,256]{1,0:T(8,128)(2,1)}, f32[256,25...) custom-call(bf16[256,256]{1,0:T(8,128)(2,1)S(1)} %get-tuple-element.21.refs_0_, ...), custom_call_target="tpu_custom_call" | custom-call | tf_op jit(solution)/shard_map/deliver/pallas_call | solution.py:606

commit v10 on v8

--- a/solution.py
+++ b/solution.py
@@ -438,7 +438,7 @@
     r.send_s[:, :, 128:] = r.send_s[:, :, 128:] + packed_rows(nseq, group, {0: peak})
     send_all("s", nseq - 1)
     r.send_f[...], peak = encode(scale * inverse(r.spec_p, r.spec_g, True))
-    send_all("f")
+    send_all("f", nseq - 1)
     r.send_fs[...] = packed_rows(nseq, group, {0: peak})
     send_all("fs")
 

time: 43 us -> 43 us (level)
  no operation moved by 1% of the time
where the time goes in v10:
time: 43 us
  Pallas kernels  42.3 us (98%)
  between operations  0.64 us (1%)
    pallas_call x1, Pallas kernels, per_device(): pl.pallas_call(functools.partial(kernel, names, nseq, nchan, group, scale...  41.4 us
    pallas_call x1, Pallas kernels, per_device(): pl.pallas_call(deliver, out_shape=tuple(results.values()), in_specs=[vmem...  0.94 us

profile of v10, /device:TPU:16, one launch (start us, length us, event | category | flops | bytes accessed | tf_op | source)
XLA Modules:
  0.0 43.0 jit_solution(9300192019348363363)
XLA Ops:
  0.6 41.4 %hyena.1 = (bf16[256,256]{1,0:T(8,128)(2,1)S(1)}, bf16[256,256]{1,0:T(8,128)(2,1)S(1)}, bf16[256,256]{1,0:T(8,128)(2,1)S(1)}, bf16[256,256]{1,0:T(8,128)(2,1)S(1...) custom-call(bf16[256,256]{1,0:T(8,128)(2,1)} %refs_0_.1, bf16[256,256]{1,0:T(8,128)(2,1)} %refs_1_.1, ...), custom_call_target="tpu_custom_call" | custom-call | tf_op jit(solution)/shard_map/hyena/pallas_call | solution.py:593
  42.0 0.9 %deliver.1 = (bf16[256,256]{1,0:T(8,128)(2,1)}, bf16[256,256]{1,0:T(8,128)(2,1)}, bf16[256,256]{1,0:T(8,128)(2,1)}, bf16[256,256]{1,0:T(8,128)(2,1)}, f32[256,25...) custom-call(bf16[256,256]{1,0:T(8,128)(2,1)S(1)} %get-tuple-element.21.refs_0_, ...), custom_call_target="tpu_custom_call" | custom-call | tf_op jit(solution)/shard_map/deliver/pallas_call | solution.py:604
